TPU v7x, 128 devices: a whole 4x4x4 slice. The times are simulated.
128 devices in a mesh: seq: 32 (over y, x, core), head: 4 (over z).
Axes of the slice: x: 4, y: 4, z: 4, core: 2. Of those that a mesh axis runs over, the one named last changes fastest.
Arguments:
- queries: bfloat16 [4096, 16, 128], P('seq', 'head'), may hold values from -6 to 6
- keys: bfloat16 [4096, 16, 4, 128], P('seq', 'head'), may hold values from -6 to 6
- values: bfloat16 [4096, 16, 4, 128], P('seq', 'head'), may hold values from -6 to 6
- beta_logits: float32 [16, 4, 4096], P('head', None, 'seq'), may hold values from -10 to 4
- out_cot: bfloat16 [4096, 4096], P('seq', 'head'), may hold values from -6 to 6
- out_weight: bfloat16 [2048, 4096], P('head'), may hold values from -0.09375 to 0.09375
Outputs:
- query_grad: float32 [4096, 16, 128], P('seq', 'head')
- key_grad: float32 [4096, 16, 4, 128], P('seq', 'head')
- value_grad: float32 [4096, 16, 4, 128], P('seq', 'head')
- beta_grad: float32 [16, 4, 4096], P('head', None, 'seq')
All inputs are finite; a program needn't handle non-finite values.
Results may differ from a plain program's by a relative error of at most 0.00035.
Values may be sent and summed in bfloat16 or wider, within the bound.
A program may use at most 128 MiB of HBM per device.

v0:
```python
import jax
import jax.numpy as jnp
from jax import lax
from jax.sharding import PartitionSpec as P

precise = lax.Precision.HIGHEST


def shifted(value, axis, steps):
    count = lax.axis_size(axis)
    leading, last = (max(0, -steps), min(count, count - steps))
    return lax.ppermute(value, axis, [(source, source + steps) for source in range(leading, last)])


def product(left, right):
    return jnp.matmul(left, right, precision=precise)


def block_maps(query_rows, key_raw, value_rows, logit_rows):
    step_count = key_raw.shape[0]
    row_count = query_rows.shape[0]
    reflections = step_count // row_count
    head_width = key_raw.shape[1]
    key_unit = key_raw * lax.rsqrt(jnp.sum(key_raw * key_raw, axis=1, keepdims=True) + 1e-06)
    beta_values = 2.0 * jax.nn.sigmoid(logit_rows)
    key_gram = product(key_unit, key_unit.T)
    lower_part = jnp.tril(key_gram, -1)
    system = jnp.eye(step_count, dtype=jnp.float32) + beta_values[:, None] * lower_part
    right_side = beta_values[:, None] * jnp.concatenate([key_unit, value_rows], axis=1)
    solved = jax.scipy.linalg.solve_triangular(system, right_side, lower=True, unit_diagonal=True)
    w_part = solved[:, :head_width]
    u_part = solved[:, head_width:]
    scaled = query_rows * head_width ** (-0.5)
    scores = product(scaled, key_unit.T)
    token_row = lax.broadcasted_iota(jnp.int32, (row_count, step_count), 0)
    step_col = lax.broadcasted_iota(jnp.int32, (row_count, step_count), 1)
    scores = jnp.where(step_col < (token_row + 1) * reflections, scores, 0.0)
    carry_map = jnp.eye(head_width, dtype=jnp.float32) - product(key_unit.T, w_part)
    offset = product(key_unit.T, u_part)
    reader = scaled - product(scores, w_part)
    direct = product(scores, u_part)
    return (carry_map, offset, reader, direct)


def block_apply(start_state, query_rows, key_raw, value_rows, logit_rows):
    carry_map, offset, reader, direct = block_maps(query_rows, key_raw, value_rows, logit_rows)
    return (product(reader, start_state) + direct, product(carry_map, start_state) + offset)


def compose_maps(earlier, later):
    return (product(later[0], earlier[0]), product(later[0], earlier[1]) + later[1])


def local(queries, keys, values, beta_logits, out_cot, out_weight):
    token_count, head_count, head_width = queries.shape
    reflections = keys.shape[2]
    out_grad = lax.dot_general(
        lax.all_gather(out_cot, "head", axis=1, tiled=True),
        out_weight,
        (((1,), (1,)), ((), ())),
        preferred_element_type=jnp.float32,
    )
    out_grad = out_grad.reshape(token_count, head_count, head_width)
    step_count = min(128, token_count * reflections)
    row_count = step_count // reflections
    block_count = token_count // row_count
    query_blocks = (
        queries.astype(jnp.float32)
        .reshape(block_count, row_count, head_count, head_width)
        .transpose(0, 2, 1, 3)
    )
    key_blocks = keys.astype(jnp.float32).reshape(
        block_count, row_count, head_count, reflections, head_width
    )
    key_blocks = key_blocks.transpose(0, 2, 1, 3, 4).reshape(
        block_count, head_count, step_count, head_width
    )
    value_blocks = values.astype(jnp.float32).reshape(
        block_count, row_count, head_count, reflections, head_width
    )
    value_blocks = value_blocks.transpose(0, 2, 1, 3, 4).reshape(
        block_count, head_count, step_count, head_width
    )
    logit_blocks = beta_logits.reshape(head_count, reflections, block_count, row_count)
    logit_blocks = logit_blocks.transpose(2, 0, 3, 1).reshape(block_count, head_count, step_count)
    grad_blocks = out_grad.reshape(block_count, row_count, head_count, head_width).transpose(
        0, 2, 1, 3
    )
    carry_maps, offsets, readers, directs = jax.vmap(jax.vmap(block_maps))(
        query_blocks, key_blocks, value_blocks, logit_blocks
    )
    maps_back = carry_maps.transpose(0, 1, 3, 2)
    sources = product(readers.transpose(0, 1, 3, 2), grad_blocks)
    identity_map = jnp.broadcast_to(
        jnp.eye(head_width, dtype=jnp.float32), (head_count, head_width, head_width)
    )
    zero_state = jnp.zeros((head_count, head_width, head_width), jnp.float32)

    def fold_block(running, element):
        return (compose_maps(running, element), None)

    group_forward, unused_one = lax.scan(
        fold_block, (identity_map, zero_state), (carry_maps, offsets)
    )
    group_backward, unused_two = lax.scan(
        fold_block, (identity_map, zero_state), (maps_back, sources), reverse=True
    )
    seq_count = lax.axis_size("seq")

    def both_turn(turn_index, carried):
        state_now, adjoint_now = carried
        state_next = shifted(product(group_forward[0], state_now) + group_forward[1], "seq", 1)
        adjoint_next = shifted(
            product(group_backward[0], adjoint_now) + group_backward[1], "seq", -1
        )
        return (state_next, adjoint_next)

    entry_state, exit_adjoint = lax.fori_loop(0, seq_count - 1, both_turn, (zero_state, zero_state))

    def walk_forward(carried, element):
        return (product(element[0], carried) + element[1], carried)

    unused_three, starts = lax.scan(walk_forward, entry_state, (carry_maps, offsets))
    unused_four, block_ends = lax.scan(
        walk_forward, exit_adjoint, (maps_back, sources), reverse=True
    )

    def grad_block(start_state, query_rows, key_raw, value_rows, logit_rows, out_rows, end_adjoint):
        unused_out, pull_back = jax.vjp(
            block_apply, start_state, query_rows, key_raw, value_rows, logit_rows
        )
        return pull_back((out_rows, end_adjoint))[1:]

    query_part, key_part, value_part, logit_part = jax.vmap(jax.vmap(grad_block))(
        starts, query_blocks, key_blocks, value_blocks, logit_blocks, grad_blocks, block_ends
    )
    query_grad = query_part.transpose(0, 2, 1, 3).reshape(token_count, head_count, head_width)
    key_grad = key_part.reshape(block_count, head_count, row_count, reflections, head_width)
    key_grad = key_grad.transpose(0, 2, 1, 3, 4).reshape(
        token_count, head_count, reflections, head_width
    )
    value_grad = value_part.reshape(block_count, head_count, row_count, reflections, head_width)
    value_grad = value_grad.transpose(0, 2, 1, 3, 4).reshape(
        token_count, head_count, reflections, head_width
    )
    beta_grad = logit_part.reshape(block_count, head_count, row_count, reflections)
    beta_grad = beta_grad.transpose(1, 3, 0, 2).reshape(head_count, reflections, token_count)
    return (query_grad, key_grad, value_grad, beta_grad)


def solution(mesh):
    return jax.shard_map(
        local,
        mesh=mesh,
        in_specs=(
            P("seq", "head", None),
            P("seq", "head", None, None),
            P("seq", "head", None, None),
            P("head", None, "seq"),
            P("seq", "head"),
            P("head", None),
        ),
        out_specs=(
            P("seq", "head", None),
            P("seq", "head", None, None),
            P("seq", "head", None, None),
            P("head", None, "seq"),
        ),
        check_vma=False,
    )
```

profile of v0, /device:TPU:1, one launch (start us, length us, event | category | flops | bytes accessed | tf_op | source)
XLA Modules:
  0.0 837.3 jit_solution(11183096544797838511)
XLA Ops:
  15.0 158.1 %custom-call.13 = f32[4,4,1,128,128]{3,4,2,1,0:T(8,128)} custom-call(f32[4,4,1,128,128]{4,3,2,1,0:T(8,128)S(1)} %add_bitcast_fusion), custom_call_target="InvertDiagBlocksLowerTriangular" | custom-call | tf_op jit(solution)/shard_map/vmap(vmap(jit(_solve_triangular)))/triangular_solve/custom-call.1 | solution.py:30
  174.6 4.0 fusion.28
  178.6 3.1 fusion.47
  192.7 18.1 %while.73 = (s32[]{:T(128)}, f32[4,128,128]{2,1,0:T(8,128)S(1)}, f32[4,128,128]{2,1,0:T(8,128)}, f32[4,4,128,128]{3,2,1,0:T(8,128)}, f32[4,4,128,128]{3,2,1,0:T(8,128)}, /*index=5*/s32[]{:T(128)}, s32[]{:T(128)}) while((s32[]{:T(128)}, f32[4,128,128]{2,1,0:T(8,128)S(1)}, f32[4,128,128]{2,1,0:T(8,128)}, ...), condition=%wide.region_2.4_spmd.clone, body=%wide.region_1.3_spmd.clone.sunk | while | flops 201457664 | bytes 2885207 | solution.py:102
  210.9 4.8 fusion.89
  217.5 3.8 fusion.63
  221.3 3.8 fusion.68
  225.2 17.8 %while.74 = (s32[]{:T(128)}, f32[4,128,128]{2,1,0:T(8,128)S(1)}, f32[4,128,128]{2,1,0:T(8,128)}, f32[4,4,128,128]{3,2,1,0:T(8,128)}, f32[4,4,128,128]{3,2,1,0:T(8,128)}, /*index=5*/s32[]{:T(128)}, s32[]{:T(128)}, s32[]{:T(128)}) while((s32[]{:T(128)}, f32[4,128,128]{2,1,0:T(8,128)S(1)}, f32[4,128,128]{2,1,0:T(8,128)}, ...), condition=%wide.region_4.6_spmd.clone, body=%wide.region_3.5_spmd.clone.sunk | while | flops 201457664 | bytes 2885230 | solution.py:105
  244.5 504.6 %while.70 = (s32[]{:T(128)}, f32[4,128,128]{2,1,0:T(8,128)}, f32[4,128,128]{2,1,0:T(8,128)}, f32[4,128,128]{2,1,0:T(8,128)}, f32[4,128,128]{2,1,0:T(8,128)}, /*i...) while((s32[]{:T(128)}, f32[4,128,128]{2,1,0:T(8,128)}, f32[4,128,128]{2,1,0:T(8,128)}, ...), condition=%wide.region_6.8_spmd, body=%wide.region_5.7_spmd.sunk | while | flops 201457664 | bytes 4194469 | solution.py:118
  246.7 4.5 collective-permute-start
  255.3 6.1 collective-permute-done.1
  270.8 4.9 collective-permute-done.1
  285.1 4.9 collective-permute-done.1
  299.4 6.3 collective-permute-done.1
  315.1 7.0 collective-permute-done.1
  331.5 7.0 collective-permute-done.1
  348.0 7.0 collective-permute-done.1
  364.4 7.0 collective-permute-done.1
  380.8 7.0 collective-permute-done.1
  397.2 7.0 collective-permute-done.1
  413.6 7.0 collective-permute-done.1
  430.1 7.0 collective-permute-done.1
  446.5 7.0 collective-permute-done.1
  462.9 7.0 collective-permute-done.1
  479.3 7.0 collective-permute-done.1
  495.7 7.0 collective-permute-done.1
  512.2 7.0 collective-permute-done.1
  528.6 7.0 collective-permute-done.1
  545.0 7.0 collective-permute-done.1
  561.4 7.0 collective-permute-done.1
  577.9 7.0 collective-permute-done.1
  594.3 7.0 collective-permute-done.1
  610.7 7.0 collective-permute-done.1
  627.1 7.0 collective-permute-done.1
  643.5 7.0 collective-permute-done.1
  660.0 7.0 collective-permute-done.1
  676.4 7.0 collective-permute-done.1
  692.8 7.0 collective-permute-done.1
  709.2 7.0 collective-permute-done.1
  725.6 7.0 collective-permute-done.1
  742.1 7.0 collective-permute-done.1
  750.2 15.2 %while.72 = (s32[]{:T(128)}, f32[4,128,128]{2,1,0:T(8,128)}, f32[4,4,128,128]{3,2,1,0:T(8,128)}, f32[4,4,128,128]{3,2,1,0:T(8,128)}, f32[4,4,128,128]{3,2,1,0:T(8,128)}, /*index=5*/s32[]{:T(128)}, s32[]{:T(128)}) while((s32[]{:T(128)}, f32[4,128,128]{2,1,0:T(8,128)}, f32[4,4,128,128]{3,2,1,0:T(8,128)}, f32[4,4,128,128]{3,2,1,0:T(8,128)}, ...), condition=%wide.region_10.12_spmd, body=%wide.region_9.11_spmd.sunk | while | flops 100728832 | bytes 2098269 | solution.py:124
  766.6 15.7 %while.71 = (s32[]{:T(128)}, f32[4,128,128]{2,1,0:T(8,128)}, f32[4,4,128,128]{3,2,1,0:T(8,128)}, f32[4,4,128,128]{3,2,1,0:T(8,128)}, f32[4,4,128,128]{3,2,1,0:T(8,128)}, /*index=5*/s32[]{:T(128)}) while((s32[]{:T(128)}, f32[4,128,128]{2,1,0:T(8,128)}, f32[4,4,128,128]{3,2,1,0:T(8,128)}, f32[4,4,128,128]{3,2,1,0:T(8,128)}, ...), condition=%wide.region_8.10_spmd, body=%wide.region_7.9_spmd.sunk | while | flops 100728832 | bytes 2098757 | solution.py:123
  785.4 3.6 convolution_negate_fusion.1
  795.7 3.5 multiply_reduce_fusion
  799.1 3.4 fusion.43
  810.0 3.3 multiply_reduce_fusion.1
  818.0 4.0 fusion.33
  (316 shorter events, 409.8 us)
Async XLA Ops:
  7.2 203.7 %all-gather.2.cloned.1.call-start = ((), (), s32[]{:S(2)}) async-start(), calls=%async_computation | async-start | bytes 1310720 | tf_op jit(solution)/shard_map/all_gather | solution.py:58
  246.7 8.6 %collective-permute-start = (f32[4,128,128]{2,1,0:T(8,128)}, f32[4,128,128]{2,1,0:T(8,128)}, u32[]{:S(2)}, u32[]{:S(2)}) collective-permute-start(f32[4,128,128]{2,1,0:T(8,128)} %convolution_add_fusion.19), channel_id=1, source_target_pairs={{0,4},{4,8},{8,12},{12,16},{16,20},{20,24},{24,28},{28,32},{32,36}... | collective-permute-start | bytes 786440 | tf_op jit(solution)/shard_map/while/body/eval_jaxpr/ppermute | solution.py:12
  253.4 8.0 collective-permute-start.1
  267.7 8.0 collective-permute-start.1
  277.9 7.2 collective-permute-start
  282.0 8.0 collective-permute-start.1
  296.3 9.4 %collective-permute-start.1 = (f32[4,128,128]{2,1,0:T(8,128)}, f32[4,128,128]{2,1,0:T(8,128)}, u32[]{:S(2)}, u32[]{:S(2)}) collective-permute-start(f32[4,128,128]{2,1,0:T(8,128)} %convolution_add_fusion.20), channel_id=1, source_target_pairs={{4,0},{8,4},{12,8},{16,12},{20,16},{24,20},{28,24},{32,28},{36,32}... | collective-permute-start | bytes 786440 | tf_op jit(solution)/shard_map/while/body/eval_jaxpr/ppermute | solution.py:12
  307.9 7.2 collective-permute-start
  312.0 10.1 %collective-permute-start.1 = (f32[4,128,128]{2,1,0:T(8,128)}, f32[4,128,128]{2,1,0:T(8,128)}, u32[]{:S(2)}, u32[]{:S(2)}) collective-permute-start(f32[4,128,128]{2,1,0:T(8,128)} %convolution_add_fusion.20), channel_id=1, source_target_pairs={{4,0},{8,4},{12,8},{16,12},{20,16},{24,20},{28,24},{32,28},{36,32}... | collective-permute-start | bytes 786440 | tf_op jit(solution)/shard_map/while/body/eval_jaxpr/ppermute | solution.py:12
  324.4 7.2 collective-permute-start
  328.4 10.1 %collective-permute-start.1 = (f32[4,128,128]{2,1,0:T(8,128)}, f32[4,128,128]{2,1,0:T(8,128)}, u32[]{:S(2)}, u32[]{:S(2)}) collective-permute-start(f32[4,128,128]{2,1,0:T(8,128)} %convolution_add_fusion.20), channel_id=1, source_target_pairs={{4,0},{8,4},{12,8},{16,12},{20,16},{24,20},{28,24},{32,28},{36,32}... | collective-permute-start | bytes 786440 | tf_op jit(solution)/shard_map/while/body/eval_jaxpr/ppermute | solution.py:12
  340.8 7.2 collective-permute-start
  344.9 10.1 %collective-permute-start.1 = (f32[4,128,128]{2,1,0:T(8,128)}, f32[4,128,128]{2,1,0:T(8,128)}, u32[]{:S(2)}, u32[]{:S(2)}) collective-permute-start(f32[4,128,128]{2,1,0:T(8,128)} %convolution_add_fusion.20), channel_id=1, source_target_pairs={{4,0},{8,4},{12,8},{16,12},{20,16},{24,20},{28,24},{32,28},{36,32}... | collective-permute-start | bytes 786440 | tf_op jit(solution)/shard_map/while/body/eval_jaxpr/ppermute | solution.py:12
  357.2 7.2 collective-permute-start
  361.3 10.1 %collective-permute-start.1 = (f32[4,128,128]{2,1,0:T(8,128)}, f32[4,128,128]{2,1,0:T(8,128)}, u32[]{:S(2)}, u32[]{:S(2)}) collective-permute-start(f32[4,128,128]{2,1,0:T(8,128)} %convolution_add_fusion.20), channel_id=1, source_target_pairs={{4,0},{8,4},{12,8},{16,12},{20,16},{24,20},{28,24},{32,28},{36,32}... | collective-permute-start | bytes 786440 | tf_op jit(solution)/shard_map/while/body/eval_jaxpr/ppermute | solution.py:12
  377.7 10.1 %collective-permute-start.1 = (f32[4,128,128]{2,1,0:T(8,128)}, f32[4,128,128]{2,1,0:T(8,128)}, u32[]{:S(2)}, u32[]{:S(2)}) collective-permute-start(f32[4,128,128]{2,1,0:T(8,128)} %convolution_add_fusion.20), channel_id=1, source_target_pairs={{4,0},{8,4},{12,8},{16,12},{20,16},{24,20},{28,24},{32,28},{36,32}... | collective-permute-start | bytes 786440 | tf_op jit(solution)/shard_map/while/body/eval_jaxpr/ppermute | solution.py:12
  390.0 7.2 collective-permute-start
  394.1 10.1 %collective-permute-start.1 = (f32[4,128,128]{2,1,0:T(8,128)}, f32[4,128,128]{2,1,0:T(8,128)}, u32[]{:S(2)}, u32[]{:S(2)}) collective-permute-start(f32[4,128,128]{2,1,0:T(8,128)} %convolution_add_fusion.20), channel_id=1, source_target_pairs={{4,0},{8,4},{12,8},{16,12},{20,16},{24,20},{28,24},{32,28},{36,32}... | collective-permute-start | bytes 786440 | tf_op jit(solution)/shard_map/while/body/eval_jaxpr/ppermute | solution.py:12
  410.5 10.1 %collective-permute-start.1 = (f32[4,128,128]{2,1,0:T(8,128)}, f32[4,128,128]{2,1,0:T(8,128)}, u32[]{:S(2)}, u32[]{:S(2)}) collective-permute-start(f32[4,128,128]{2,1,0:T(8,128)} %convolution_add_fusion.20), channel_id=1, source_target_pairs={{4,0},{8,4},{12,8},{16,12},{20,16},{24,20},{28,24},{32,28},{36,32}... | collective-permute-start | bytes 786440 | tf_op jit(solution)/shard_map/while/body/eval_jaxpr/ppermute | solution.py:12
  427.0 10.1 %collective-permute-start.1 = (f32[4,128,128]{2,1,0:T(8,128)}, f32[4,128,128]{2,1,0:T(8,128)}, u32[]{:S(2)}, u32[]{:S(2)}) collective-permute-start(f32[4,128,128]{2,1,0:T(8,128)} %convolution_add_fusion.20), channel_id=1, source_target_pairs={{4,0},{8,4},{12,8},{16,12},{20,16},{24,20},{28,24},{32,28},{36,32}... | collective-permute-start | bytes 786440 | tf_op jit(solution)/shard_map/while/body/eval_jaxpr/ppermute | solution.py:12
  439.3 7.2 collective-permute-start
  443.4 10.1 %collective-permute-start.1 = (f32[4,128,128]{2,1,0:T(8,128)}, f32[4,128,128]{2,1,0:T(8,128)}, u32[]{:S(2)}, u32[]{:S(2)}) collective-permute-start(f32[4,128,128]{2,1,0:T(8,128)} %convolution_add_fusion.20), channel_id=1, source_target_pairs={{4,0},{8,4},{12,8},{16,12},{20,16},{24,20},{28,24},{32,28},{36,32}... | collective-permute-start | bytes 786440 | tf_op jit(solution)/shard_map/while/body/eval_jaxpr/ppermute | solution.py:12
  459.8 10.1 %collective-permute-start.1 = (f32[4,128,128]{2,1,0:T(8,128)}, f32[4,128,128]{2,1,0:T(8,128)}, u32[]{:S(2)}, u32[]{:S(2)}) collective-permute-start(f32[4,128,128]{2,1,0:T(8,128)} %convolution_add_fusion.20), channel_id=1, source_target_pairs={{4,0},{8,4},{12,8},{16,12},{20,16},{24,20},{28,24},{32,28},{36,32}... | collective-permute-start | bytes 786440 | tf_op jit(solution)/shard_map/while/body/eval_jaxpr/ppermute | solution.py:12
  476.2 10.1 %collective-permute-start.1 = (f32[4,128,128]{2,1,0:T(8,128)}, f32[4,128,128]{2,1,0:T(8,128)}, u32[]{:S(2)}, u32[]{:S(2)}) collective-permute-start(f32[4,128,128]{2,1,0:T(8,128)} %convolution_add_fusion.20), channel_id=1, source_target_pairs={{4,0},{8,4},{12,8},{16,12},{20,16},{24,20},{28,24},{32,28},{36,32}... | collective-permute-start | bytes 786440 | tf_op jit(solution)/shard_map/while/body/eval_jaxpr/ppermute | solution.py:12
  488.6 7.2 collective-permute-start
  492.6 10.1 %collective-permute-start.1 = (f32[4,128,128]{2,1,0:T(8,128)}, f32[4,128,128]{2,1,0:T(8,128)}, u32[]{:S(2)}, u32[]{:S(2)}) collective-permute-start(f32[4,128,128]{2,1,0:T(8,128)} %convolution_add_fusion.20), channel_id=1, source_target_pairs={{4,0},{8,4},{12,8},{16,12},{20,16},{24,20},{28,24},{32,28},{36,32}... | collective-permute-start | bytes 786440 | tf_op jit(solution)/shard_map/while/body/eval_jaxpr/ppermute | solution.py:12
  509.1 10.1 %collective-permute-start.1 = (f32[4,128,128]{2,1,0:T(8,128)}, f32[4,128,128]{2,1,0:T(8,128)}, u32[]{:S(2)}, u32[]{:S(2)}) collective-permute-start(f32[4,128,128]{2,1,0:T(8,128)} %convolution_add_fusion.20), channel_id=1, source_target_pairs={{4,0},{8,4},{12,8},{16,12},{20,16},{24,20},{28,24},{32,28},{36,32}... | collective-permute-start | bytes 786440 | tf_op jit(solution)/shard_map/while/body/eval_jaxpr/ppermute | solution.py:12
  521.4 7.2 collective-permute-start
  525.5 10.1 %collective-permute-start.1 = (f32[4,128,128]{2,1,0:T(8,128)}, f32[4,128,128]{2,1,0:T(8,128)}, u32[]{:S(2)}, u32[]{:S(2)}) collective-permute-start(f32[4,128,128]{2,1,0:T(8,128)} %convolution_add_fusion.20), channel_id=1, source_target_pairs={{4,0},{8,4},{12,8},{16,12},{20,16},{24,20},{28,24},{32,28},{36,32}... | collective-permute-start | bytes 786440 | tf_op jit(solution)/shard_map/while/body/eval_jaxpr/ppermute | solution.py:12
  537.8 7.2 collective-permute-start
  541.9 10.1 %collective-permute-start.1 = (f32[4,128,128]{2,1,0:T(8,128)}, f32[4,128,128]{2,1,0:T(8,128)}, u32[]{:S(2)}, u32[]{:S(2)}) collective-permute-start(f32[4,128,128]{2,1,0:T(8,128)} %convolution_add_fusion.20), channel_id=1, source_target_pairs={{4,0},{8,4},{12,8},{16,12},{20,16},{24,20},{28,24},{32,28},{36,32}... | collective-permute-start | bytes 786440 | tf_op jit(solution)/shard_map/while/body/eval_jaxpr/ppermute | solution.py:12
  558.3 10.1 %collective-permute-start.1 = (f32[4,128,128]{2,1,0:T(8,128)}, f32[4,128,128]{2,1,0:T(8,128)}, u32[]{:S(2)}, u32[]{:S(2)}) collective-permute-start(f32[4,128,128]{2,1,0:T(8,128)} %convolution_add_fusion.20), channel_id=1, source_target_pairs={{4,0},{8,4},{12,8},{16,12},{20,16},{24,20},{28,24},{32,28},{36,32}... | collective-permute-start | bytes 786440 | tf_op jit(solution)/shard_map/while/body/eval_jaxpr/ppermute | solution.py:12
  570.7 7.2 collective-permute-start
  574.7 10.1 %collective-permute-start.1 = (f32[4,128,128]{2,1,0:T(8,128)}, f32[4,128,128]{2,1,0:T(8,128)}, u32[]{:S(2)}, u32[]{:S(2)}) collective-permute-start(f32[4,128,128]{2,1,0:T(8,128)} %convolution_add_fusion.20), channel_id=1, source_target_pairs={{4,0},{8,4},{12,8},{16,12},{20,16},{24,20},{28,24},{32,28},{36,32}... | collective-permute-start | bytes 786440 | tf_op jit(solution)/shard_map/while/body/eval_jaxpr/ppermute | solution.py:12
  591.2 10.1 %collective-permute-start.1 = (f32[4,128,128]{2,1,0:T(8,128)}, f32[4,128,128]{2,1,0:T(8,128)}, u32[]{:S(2)}, u32[]{:S(2)}) collective-permute-start(f32[4,128,128]{2,1,0:T(8,128)} %convolution_add_fusion.20), channel_id=1, source_target_pairs={{4,0},{8,4},{12,8},{16,12},{20,16},{24,20},{28,24},{32,28},{36,32}... | collective-permute-start | bytes 786440 | tf_op jit(solution)/shard_map/while/body/eval_jaxpr/ppermute | solution.py:12
  607.6 10.1 %collective-permute-start.1 = (f32[4,128,128]{2,1,0:T(8,128)}, f32[4,128,128]{2,1,0:T(8,128)}, u32[]{:S(2)}, u32[]{:S(2)}) collective-permute-start(f32[4,128,128]{2,1,0:T(8,128)} %convolution_add_fusion.20), channel_id=1, source_target_pairs={{4,0},{8,4},{12,8},{16,12},{20,16},{24,20},{28,24},{32,28},{36,32}... | collective-permute-start | bytes 786440 | tf_op jit(solution)/shard_map/while/body/eval_jaxpr/ppermute | solution.py:12
  619.9 7.2 collective-permute-start
  624.0 10.1 %collective-permute-start.1 = (f32[4,128,128]{2,1,0:T(8,128)}, f32[4,128,128]{2,1,0:T(8,128)}, u32[]{:S(2)}, u32[]{:S(2)}) collective-permute-start(f32[4,128,128]{2,1,0:T(8,128)} %convolution_add_fusion.20), channel_id=1, source_target_pairs={{4,0},{8,4},{12,8},{16,12},{20,16},{24,20},{28,24},{32,28},{36,32}... | collective-permute-start | bytes 786440 | tf_op jit(solution)/shard_map/while/body/eval_jaxpr/ppermute | solution.py:12
  640.4 10.1 %collective-permute-start.1 = (f32[4,128,128]{2,1,0:T(8,128)}, f32[4,128,128]{2,1,0:T(8,128)}, u32[]{:S(2)}, u32[]{:S(2)}) collective-permute-start(f32[4,128,128]{2,1,0:T(8,128)} %convolution_add_fusion.20), channel_id=1, source_target_pairs={{4,0},{8,4},{12,8},{16,12},{20,16},{24,20},{28,24},{32,28},{36,32}... | collective-permute-start | bytes 786440 | tf_op jit(solution)/shard_map/while/body/eval_jaxpr/ppermute | solution.py:12
  652.8 7.2 collective-permute-start
  656.9 10.1 %collective-permute-start.1 = (f32[4,128,128]{2,1,0:T(8,128)}, f32[4,128,128]{2,1,0:T(8,128)}, u32[]{:S(2)}, u32[]{:S(2)}) collective-permute-start(f32[4,128,128]{2,1,0:T(8,128)} %convolution_add_fusion.20), channel_id=1, source_target_pairs={{4,0},{8,4},{12,8},{16,12},{20,16},{24,20},{28,24},{32,28},{36,32}... | collective-permute-start | bytes 786440 | tf_op jit(solution)/shard_map/while/body/eval_jaxpr/ppermute | solution.py:12
  669.2 7.2 collective-permute-start
  673.3 10.1 %collective-permute-start.1 = (f32[4,128,128]{2,1,0:T(8,128)}, f32[4,128,128]{2,1,0:T(8,128)}, u32[]{:S(2)}, u32[]{:S(2)}) collective-permute-start(f32[4,128,128]{2,1,0:T(8,128)} %convolution_add_fusion.20), channel_id=1, source_target_pairs={{4,0},{8,4},{12,8},{16,12},{20,16},{24,20},{28,24},{32,28},{36,32}... | collective-permute-start | bytes 786440 | tf_op jit(solution)/shard_map/while/body/eval_jaxpr/ppermute | solution.py:12
  689.7 10.1 %collective-permute-start.1 = (f32[4,128,128]{2,1,0:T(8,128)}, f32[4,128,128]{2,1,0:T(8,128)}, u32[]{:S(2)}, u32[]{:S(2)}) collective-permute-start(f32[4,128,128]{2,1,0:T(8,128)} %convolution_add_fusion.20), channel_id=1, source_target_pairs={{4,0},{8,4},{12,8},{16,12},{20,16},{24,20},{28,24},{32,28},{36,32}... | collective-permute-start | bytes 786440 | tf_op jit(solution)/shard_map/while/body/eval_jaxpr/ppermute | solution.py:12
  702.0 7.2 collective-permute-start
  706.1 10.1 %collective-permute-start.1 = (f32[4,128,128]{2,1,0:T(8,128)}, f32[4,128,128]{2,1,0:T(8,128)}, u32[]{:S(2)}, u32[]{:S(2)}) collective-permute-start(f32[4,128,128]{2,1,0:T(8,128)} %convolution_add_fusion.20), channel_id=1, source_target_pairs={{4,0},{8,4},{12,8},{16,12},{20,16},{24,20},{28,24},{32,28},{36,32}... | collective-permute-start | bytes 786440 | tf_op jit(solution)/shard_map/while/body/eval_jaxpr/ppermute | solution.py:12
  722.5 10.1 %collective-permute-start.1 = (f32[4,128,128]{2,1,0:T(8,128)}, f32[4,128,128]{2,1,0:T(8,128)}, u32[]{:S(2)}, u32[]{:S(2)}) collective-permute-start(f32[4,128,128]{2,1,0:T(8,128)} %convolution_add_fusion.20), channel_id=1, source_target_pairs={{4,0},{8,4},{12,8},{16,12},{20,16},{24,20},{28,24},{32,28},{36,32}... | collective-permute-start | bytes 786440 | tf_op jit(solution)/shard_map/while/body/eval_jaxpr/ppermute | solution.py:12
  739.0 10.1 %collective-permute-start.1 = (f32[4,128,128]{2,1,0:T(8,128)}, f32[4,128,128]{2,1,0:T(8,128)}, u32[]{:S(2)}, u32[]{:S(2)}) collective-permute-start(f32[4,128,128]{2,1,0:T(8,128)} %convolution_add_fusion.20), channel_id=1, source_target_pairs={{4,0},{8,4},{12,8},{16,12},{20,16},{24,20},{28,24},{32,28},{36,32}... | collective-permute-start | bytes 786440 | tf_op jit(solution)/shard_map/while/body/eval_jaxpr/ppermute | solution.py:12
  (37 other events, 506.2 us)
Sparse Core Ops, SparseCore 0:
  9.6 26.6 all-gather.1
where the time goes:
time: 851 us; the launch traced here: 837 us
  matrix products  249 us (29%)
  waiting for transfers between devices  212 us (25%)
  other arithmetic  163 us (19%)
  starting transfers between devices  156 us (18%)
  local copies, waits for them, and re-layouts  40 us (5%)
  between operations  14.8 us (2%)
    dot_general x106, matrix products, product(): return jnp.matmul(left, right, precision=precise)  231 us
    ppermute x62, waiting for transfers between devices, shifted(): lax.ppermute(value, axis, [(source, source + steps) for source in range(l...  211 us
    another operation x4, other arithmetic, block_maps(): jax.scipy.linalg.solve_triangular(system, right_side, lower=True, unit_di...  159 us
    ppermute x62, starting transfers between devices, shifted(): lax.ppermute(value, axis, [(source, source + steps) for source in range(l...  156 us
  transfers between devices with their start and end apart: 63, of which 31 were waited for; matrix products, arithmetic and copies ran while one was open for 32% of the time, Pallas kernels for 0%

commit v1 on v0

v1 whole, which is shorter than its diff:
```python
import jax
import jax.numpy as jnp
from jax import lax
from jax.experimental import pallas as pl
from jax.experimental.pallas import tpu as pltpu
from jax.sharding import PartitionSpec as P

F32 = jnp.float32
BF16 = jnp.bfloat16
MESH = pl.DeviceIdType.MESH
HD = 128
BLK = 128
NT = (((1,), (1,)), ((), ()))
NN = (((1,), (0,)), ((), ()))


def dg(a, b, dims):
    return lax.dot_general(a, b, dims, preferred_element_type=F32)


def split(x):
    hi = x.astype(BF16)
    lo = (x - hi.astype(F32)).astype(BF16)
    return hi, lo


def dot2(a, bs, dims=NN):
    return dg(a, bs[0], dims) + dg(a, bs[1], dims)


def dot2l(as_, b, dims=NN):
    return dg(as_[0], b, dims) + dg(as_[1], b, dims)


def dot3(as_, bs, dims=NN):
    return dg(as_[0], bs[0], dims) + (dg(as_[0], bs[1], dims) + dg(as_[1], bs[0], dims))


def iota2(shape, axis):
    return lax.broadcasted_iota(jnp.int32, shape, axis)


def to_col(row, eye):
    return jnp.sum(jnp.where(eye, row, 0.0), axis=1, keepdims=True)


def to_row(col, eye):
    return jnp.sum(jnp.where(eye, col, 0.0), axis=0, keepdims=True)


def gather_kernel(cot_ref, full_ref, send_sem, recv_sem, own_sem):
    size = lax.axis_size("head")
    me = lax.axis_index("head")
    width = cot_ref.shape[1]
    barrier = pltpu.get_barrier_semaphore()
    for step in range(1, size):
        peer = lax.rem(me + step, size)
        pl.semaphore_signal(barrier, inc=1, device_id={"head": peer}, device_id_type=MESH)
    pl.semaphore_wait(barrier, size - 1)
    columns = pl.ds(pl.multiple_of(me * width, width), width)
    copies = []
    for step in range(1, size):
        peer = lax.rem(me + step, size)
        copy = pltpu.make_async_remote_copy(
            src_ref=cot_ref,
            dst_ref=full_ref.at[:, columns],
            send_sem=send_sem.at[step],
            recv_sem=recv_sem.at[step],
            device_id={"head": peer},
            device_id_type=MESH,
        )
        copy.start()
        copies.append(copy)
    own = pltpu.make_async_copy(cot_ref, full_ref.at[:, columns], own_sem)
    own.start()
    own.wait()
    for copy in copies:
        copy.wait()


def gather_cot(cot):
    rows, width = cot.shape
    size = lax.axis_size("head")
    return pl.pallas_call(
        gather_kernel,
        out_shape=jax.ShapeDtypeStruct((rows, width * size), cot.dtype),
        in_specs=[pl.BlockSpec(memory_space=pltpu.VMEM)],
        out_specs=pl.BlockSpec(memory_space=pltpu.VMEM),
        scratch_shapes=[
            pltpu.SemaphoreType.DMA((size,)),
            pltpu.SemaphoreType.DMA((size,)),
            pltpu.SemaphoreType.DMA,
        ],
        compiler_params=pltpu.CompilerParams(collective_id=0, has_side_effects=True),
        name="gather_cot",
    )(cot)


def block_scalars(k_ref, lg_ref, b, eye):
    kb = k_ref[0, b * BLK : (b + 1) * BLK, :]
    kf = kb.astype(F32)
    rs_col = lax.rsqrt(jnp.sum(kf * kf, axis=1, keepdims=True) + 1e-06)
    beta_row = 2.0 / (1.0 + jnp.exp(-lg_ref[0, b : b + 1, :]))
    beta_col = to_col(beta_row, eye)
    return kb, kf, rs_col, beta_col


def maps_kernel(q_ref, k_ref, v_ref, lg_ref, g_ref, maps_ref, fa_ref, fb_ref, ba_ref, bb_ref):
    count = k_ref.shape[1] // BLK
    tokens = q_ref.shape[0] // count
    refl = BLK // tokens
    scale = HD ** (-0.5)
    row = iota2((BLK, BLK), 0)
    col = iota2((BLK, BLK), 1)
    eye = row == col
    eye_f = jnp.where(eye, 1.0, 0.0)
    zero = jnp.zeros((BLK, HD), F32)
    scal, lower, inv = [], [], []
    for b in range(count):
        kb, kf, rs_col, beta_col = block_scalars(k_ref, lg_ref, b, eye)
        rs_row = to_row(rs_col, eye)
        gram = dg(kb, kb, NT)
        n = jnp.where(col < row, gram * (rs_col * beta_col) * rs_row, 0.0)
        scal.append((kb, rs_col, beta_col, kb.T))
        lower.append(n)

    def level(s):
        same = (row // (2 * s)) == (col // (2 * s))
        return same & ((row // s) % 2 == 1) & ((col // s) % 2 == 0)

    mask = level(1)
    for b in range(count):
        inv.append(eye_f - jnp.where(mask, lower[b], 0.0))
    s = 2
    while s < BLK:
        mask = level(s)
        for b in range(count):
            xs = split(inv[b])
            y = dot3(xs, split(jnp.where(mask, lower[b], 0.0)))
            inv[b] = inv[b] - dot3(split(y), xs)
        s *= 2
    invs = [split(x) for x in inv]

    state = jnp.concatenate([eye_f, zero], axis=1)
    for b in range(count):
        kb, rs_col, beta_col, kt = scal[b]
        vb = v_ref[0, b * BLK : (b + 1) * BLK, :].astype(F32)
        y = jnp.concatenate([zero, vb], axis=1) - rs_col * dot2(kb, split(state))
        d = dot3(invs[b], split(beta_col * y))
        fa_ref[0, b, 0] = state[:, :HD]
        fb_ref[0, b, 0] = state[:, HD:]
        fa_ref[0, b, 1] = d[:, :HD]
        fb_ref[0, b, 1] = d[:, HD:]
        state = state + dot2(kt, split(rs_col * d))
    maps_ref[0, 0] = state[:, :HD]
    maps_ref[0, 1] = state[:, HD:]

    step_tok = iota2((BLK, tokens), 0) // refl
    tok = iota2((BLK, tokens), 1)
    seen = step_tok <= tok
    state = jnp.concatenate([eye_f, zero], axis=1)
    for b in reversed(range(count)):
        kb, rs_col, beta_col, kt = scal[b]
        qb = q_ref[b * tokens : (b + 1) * tokens, :]
        gs = split(g_ref[b * tokens : (b + 1) * tokens, :])
        sc_t = jnp.where(seen, dg(kb, qb, NT) * (rs_col * scale), 0.0)
        direct = dot3(split(sc_t), gs)
        dd = rs_col * dot2(kb, split(state)) + jnp.concatenate([zero, direct], axis=1)
        f = dot3((invs[b][0].T, invs[b][1].T), split(dd))
        ba_ref[0, b, 0] = state[:, :HD]
        bb_ref[0, b, 0] = state[:, HD:]
        ba_ref[0, b, 1] = f[:, :HD]
        bb_ref[0, b, 1] = f[:, HD:]
        source = dot2(qb.T, gs) * scale
        state = (
            state
            + jnp.concatenate([zero, source], axis=1)
            - dot2(kt, split((rs_col * beta_col) * f))
        )
    maps_ref[1, 0] = state[:, :HD]
    maps_ref[1, 1] = state[:, HD:]


def head_maps(q, k, v, lg, g):
    heads, steps, _ = k.shape
    count = steps // BLK
    rows = q.shape[0]
    saved = jax.ShapeDtypeStruct((heads, count, 2, BLK, HD), F32)
    saved_spec = pl.BlockSpec((1, count, 2, BLK, HD), lambda h: (h, 0, 0, 0, 0))
    return pl.pallas_call(
        maps_kernel,
        grid=(heads,),
        out_shape=(jax.ShapeDtypeStruct((2 * heads, 2, HD, HD), F32),) + (saved,) * 4,
        in_specs=[
            pl.BlockSpec((rows, HD), lambda h: (0, h)),
            pl.BlockSpec((1, steps, HD), lambda h: (h, 0, 0)),
            pl.BlockSpec((1, steps, HD), lambda h: (h, 0, 0)),
            pl.BlockSpec((1, count, BLK), lambda h: (h, 0, 0)),
            pl.BlockSpec((rows, HD), lambda h: (0, h)),
        ],
        out_specs=(pl.BlockSpec((2, 2, HD, HD), lambda h: (h, 0, 0, 0)),) + (saved_spec,) * 4,
        name="head_maps",
    )(q, k, v, lg, g)


def scan_kernel(maps_ref, out_ref, rbuf, pref, total, entry_in, chain_out, entries,
                send_sem, recv_sem, own_sem, chain_send, chain_recv, back_send, back_recv):
    lanes = maps_ref.shape[0]
    seq = lax.axis_size("seq")
    rows = seq // lanes
    index = lax.axis_index("seq")
    line = index // lanes
    me = lax.rem(index, lanes)
    back = lax.rem(me, 2)
    base = line * lanes
    first = back * (rows - 1)
    last = (1 - back) * (rows - 1)
    ahead = lax.rem(line + 1 - 2 * back + rows, rows)
    behind = lax.rem(line - 1 + 2 * back + rows, rows)

    barrier = pltpu.get_barrier_semaphore()
    for step in range(1, lanes):
        peer = base + lax.rem(me + step, lanes)
        pl.semaphore_signal(barrier, inc=1, device_id={"seq": peer}, device_id_type=MESH)
    for other in (ahead, behind):
        pl.semaphore_signal(
            barrier, inc=1, device_id={"seq": other * lanes + me}, device_id_type=MESH
        )
    pl.semaphore_wait(barrier, lanes + 1)

    outgoing = []
    for step in range(1, lanes):
        peer = lax.rem(me + step, lanes)
        copy = pltpu.make_async_remote_copy(
            src_ref=maps_ref.at[peer],
            dst_ref=rbuf.at[me],
            send_sem=send_sem.at[step],
            recv_sem=recv_sem.at[me],
            device_id={"seq": base + peer},
            device_id_type=MESH,
        )
        copy.start()
        outgoing.append(copy)
    own = pltpu.make_async_copy(maps_ref.at[me], rbuf.at[me], own_sem)
    own.start()

    row = iota2((HD, HD), 0)
    col = iota2((HD, HD), 1)
    total[:, :HD] = jnp.where(row == col, 1.0, 0.0)
    total[:, HD:] = jnp.zeros((HD, HD), F32)

    def advance(step, carry):
        source = step + back * (lanes - 1 - 2 * step)

        @pl.when(source == me)
        def wait_own():
            pltpu.make_async_copy(maps_ref.at[me], rbuf.at[me], own_sem).wait()

        @pl.when(source != me)
        def wait_other():
            pltpu.make_async_remote_copy(
                src_ref=maps_ref.at[source],
                dst_ref=rbuf.at[source],
                send_sem=send_sem.at[0],
                recv_sem=recv_sem.at[source],
                device_id={"seq": base + source},
                device_id_type=MESH,
            ).wait_recv()

        now = total[...]
        pref[source] = now
        moved = dot3(split(rbuf[source, 0]), split(now))
        total[:, :HD] = moved[:, :HD]
        total[:, HD:] = moved[:, HD:] + rbuf[source, 1]
        return carry

    lax.fori_loop(0, lanes, advance, 0)

    chain = pltpu.make_async_remote_copy(
        src_ref=chain_out,
        dst_ref=entry_in,
        send_sem=chain_send,
        recv_sem=chain_recv,
        device_id={"seq": ahead * lanes + me},
        device_id_type=MESH,
    )

    @pl.when(line == first)
    def start_zero():
        entry_in[...] = jnp.zeros((HD, HD), F32)

    @pl.when(line != first)
    def start_chain():
        chain.wait_recv()

    states = split(entry_in[...])

    @pl.when(line != last)
    def pass_on():
        chain_out[...] = dot3(split(total[:, :HD]), states) + total[:, HD:]
        chain.start()

    def finish(step, carry):
        entries[step] = dot3(split(pref[step, :, :HD]), states) + pref[step, :, HD:]
        return carry

    lax.fori_loop(0, lanes, finish, 0)
    returning = []
    for step in range(1, lanes):
        peer = lax.rem(me + step, lanes)
        copy = pltpu.make_async_remote_copy(
            src_ref=entries.at[peer],
            dst_ref=out_ref.at[me],
            send_sem=back_send.at[step],
            recv_sem=back_recv.at[step],
            device_id={"seq": base + peer},
            device_id_type=MESH,
        )
        copy.start()
        returning.append(copy)
    out_ref[me] = entries[me]
    for copy in outgoing:
        copy.wait_send()

    @pl.when(line != last)
    def sent_on():
        chain.wait_send()

    for copy in returning:
        copy.wait()


def scan_states(maps):
    lanes = maps.shape[0]
    return pl.pallas_call(
        scan_kernel,
        out_shape=jax.ShapeDtypeStruct((lanes, HD, HD), F32),
        in_specs=[pl.BlockSpec(memory_space=pltpu.VMEM)],
        out_specs=pl.BlockSpec(memory_space=pltpu.VMEM),
        scratch_shapes=[
            pltpu.VMEM((lanes, 2, HD, HD), F32),
            pltpu.VMEM((lanes, HD, 2 * HD), F32),
            pltpu.VMEM((HD, 2 * HD), F32),
            pltpu.VMEM((HD, HD), F32),
            pltpu.VMEM((HD, HD), F32),
            pltpu.VMEM((lanes, HD, HD), F32),
            pltpu.SemaphoreType.DMA((lanes,)),
            pltpu.SemaphoreType.DMA((lanes,)),
            pltpu.SemaphoreType.DMA,
            pltpu.SemaphoreType.DMA,
            pltpu.SemaphoreType.DMA,
            pltpu.SemaphoreType.DMA((lanes,)),
            pltpu.SemaphoreType.DMA((lanes,)),
        ],
        compiler_params=pltpu.CompilerParams(collective_id=1, has_side_effects=True),
        name="scan_states",
    )(maps)


def grads_kernel(q_ref, k_ref, lg_ref, g_ref, ent_ref, fa_ref, fb_ref, ba_ref, bb_ref,
                 qg_ref, kg_ref, vg_ref, lg_out_ref):
    count = k_ref.shape[1] // BLK
    tokens = q_ref.shape[0] // count
    refl = BLK // tokens
    scale = HD ** (-0.5)
    row = iota2((BLK, BLK), 0)
    col = iota2((BLK, BLK), 1)
    eye = row == col
    seen = (iota2((tokens, BLK), 1) // refl) <= iota2((tokens, BLK), 0)
    begin = split(ent_ref[0])
    final = split(ent_ref[1])
    for b in range(count):
        kb, kf, rs_col, beta_col = block_scalars(k_ref, lg_ref, b, eye)
        rs_row = to_row(rs_col, eye)
        s0 = dot3(split(fa_ref[0, b, 0]), begin) + fb_ref[0, b, 0]
        delta = dot3(split(fa_ref[0, b, 1]), begin) + fb_ref[0, b, 1]
        lam = dot3(split(ba_ref[0, b, 0]), final) + bb_ref[0, b, 0]
        f = dot3(split(ba_ref[0, b, 1]), final) + bb_ref[0, b, 1]
        e = beta_col * f
        dlog = jnp.sum(f * delta, axis=1, keepdims=True) * (1.0 - 0.5 * beta_col)
        lg_out_ref[0, b : b + 1, :] = to_row(dlog, eye)
        vg_ref[0, b * BLK : (b + 1) * BLK, :] = e
        qb = q_ref[b * tokens : (b + 1) * tokens, :]
        gs = split(g_ref[b * tokens : (b + 1) * tokens, :])
        ds = split(delta)
        es = split(e)
        ss = split(s0)
        ls = split(lam)
        dsc = jnp.where(seen, dot3(gs, ds, NT), 0.0)
        qg_ref[b * tokens : (b + 1) * tokens, :] = scale * (
            dot3(gs, ss, NT) + dot2l(split(dsc * rs_row), kb)
        )
        m = jnp.where(col < row, dot3(es, ds, NT), 0.0)
        sym = (m + m.T) * rs_row
        dk = (
            dot3(ds, ls, NT)
            - dot3(es, ss, NT)
            + dot2l(split(dsc.T * scale), qb)
            - dot2l(split(sym), kb)
        )
        ku = kf * rs_col
        along = jnp.sum(ku * dk, axis=1, keepdims=True)
        kg_ref[0, b * BLK : (b + 1) * BLK, :] = rs_col * (dk - ku * along)


def head_grads(q, k, lg, g, entry, saved):
    heads, steps, _ = k.shape
    count = steps // BLK
    rows = q.shape[0]
    saved_spec = pl.BlockSpec((1, count, 2, BLK, HD), lambda h: (h, 0, 0, 0, 0))
    return pl.pallas_call(
        grads_kernel,
        grid=(heads,),
        out_shape=(
            jax.ShapeDtypeStruct((rows, heads * HD), F32),
            jax.ShapeDtypeStruct((heads, steps, HD), F32),
            jax.ShapeDtypeStruct((heads, steps, HD), F32),
            jax.ShapeDtypeStruct((heads, count, BLK), F32),
        ),
        in_specs=[
            pl.BlockSpec((rows, HD), lambda h: (0, h)),
            pl.BlockSpec((1, steps, HD), lambda h: (h, 0, 0)),
            pl.BlockSpec((1, count, BLK), lambda h: (h, 0, 0)),
            pl.BlockSpec((rows, HD), lambda h: (0, h)),
            pl.BlockSpec((2, HD, HD), lambda h: (h, 0, 0)),
        ]
        + [saved_spec] * 4,
        out_specs=(
            pl.BlockSpec((rows, HD), lambda h: (0, h)),
            pl.BlockSpec((1, steps, HD), lambda h: (h, 0, 0)),
            pl.BlockSpec((1, steps, HD), lambda h: (h, 0, 0)),
            pl.BlockSpec((1, count, BLK), lambda h: (h, 0, 0)),
        ),
        name="head_grads",
    )(q, k, lg, g, entry, *saved)


def local(queries, keys, values, beta_logits, out_cot, out_weight):
    rows, heads, width = queries.shape
    refl = keys.shape[2]
    steps = rows * refl
    count = steps // BLK
    out_grad = lax.dot_general(
        gather_cot(out_cot), out_weight, NT, preferred_element_type=F32
    )
    q = queries.reshape(rows, heads * width)
    k = keys.transpose(1, 0, 2, 3).reshape(heads, steps, width)
    v = values.transpose(1, 0, 2, 3).reshape(heads, steps, width)
    lg = beta_logits.transpose(0, 2, 1).reshape(heads, count, BLK)
    maps, *saved = head_maps(q, k, v, lg, out_grad)
    entry = scan_states(maps)
    qg, kg, vg, lgg = head_grads(q, k, lg, out_grad, entry, saved)
    query_grad = qg.reshape(rows, heads, width)
    key_grad = kg.reshape(heads, rows, refl, width).transpose(1, 0, 2, 3)
    value_grad = vg.reshape(heads, rows, refl, width).transpose(1, 0, 2, 3)
    beta_grad = lgg.reshape(heads, rows, refl).transpose(0, 2, 1)
    return (query_grad, key_grad, value_grad, beta_grad)


def solution(mesh):
    return jax.shard_map(
        local,
        mesh=mesh,
        in_specs=(
            P("seq", "head", None),
            P("seq", "head", None, None),
            P("seq", "head", None, None),
            P("head", None, "seq"),
            P("seq", "head"),
            P("head", None),
        ),
        out_specs=(
            P("seq", "head", None),
            P("seq", "head", None, None),
            P("seq", "head", None, None),
            P("head", None, "seq"),
        ),
        check_vma=False,
    )
```

time: 851 us -> 118 us (0.14); the launches traced: 837 us -> 117 us
  matrix products: 249 us -> 4.75 us
  waiting for transfers between devices: 212 us -> 0 us
  other arithmetic: 163 us -> 0 us
  starting transfers between devices: 156 us -> 0 us
  Pallas kernels: 0 us -> 98.5 us
  local copies, waits for them, and re-layouts: 40 us -> 13.2 us
  between operations: 14.8 us -> 0.68 us
    dot_general x108 -> x1, matrix products: 238 us -> 4.75 us  [local(): lax.dot_general(gather_cot(out_cot), out_weight, NT, preferred_element_ty...]
    ppermute x62 -> x0, waiting for transfers between devices: 211 us -> none  [shifted(): lax.ppermute(value, axis, [(source, source + steps) for source in range(l...]
    another operation x4 -> x0, other arithmetic: 159 us -> none  [block_maps(): jax.scipy.linalg.solve_triangular(system, right_side, lower=True, unit_di...]
    ppermute x62 -> x0, starting transfers between devices: 156 us -> none  [shifted(): lax.ppermute(value, axis, [(source, source + steps) for source in range(l...]
    pallas_call x0 -> x4, Pallas kernels: none -> 98.5 us  [the longest x1 36.5 us: scan_states(): pl.pallas_call(scan_kernel, out_shape=jax.ShapeDtypeStruct((lanes, HD, HD...]
    while x24 -> x0, local copies, waits for them, and re-layouts: 15.4 us -> none
    another operation x3 -> x0, matrix products: 10.8 us -> none  [block_maps(): jax.scipy.linalg.solve_triangular(system, right_side, lower=True, unit_di...]
  transfers between devices with their start and end apart: 63 -> 0, of which waited for: 31 -> 0; matrix products, arithmetic and copies ran while one was open for 32% -> 0% of each run, Pallas kernels for 0% -> 0%
where the time goes in v1:
time: 118 us; the launch traced here: 117 us
  Pallas kernels  98.5 us (83%)
  local copies, waits for them, and re-layouts  13.2 us (11%)
  matrix products  4.75 us (4%)
    pallas_call x1, Pallas kernels, scan_states(): pl.pallas_call(scan_kernel, out_shape=jax.ShapeDtypeStruct((lanes, HD, HD...  36.5 us
    pallas_call x1, Pallas kernels, head_maps(): pl.pallas_call(maps_kernel, grid=(heads,), out_shape=(jax.ShapeDtypeStruc...  29.2 us
    pallas_call x1, Pallas kernels, gather_cot(): pl.pallas_call(gather_kernel, out_shape=jax.ShapeDtypeStruct((rows, width...  19.1 us
    pallas_call x1, Pallas kernels, head_grads(): pl.pallas_call(grads_kernel, grid=(heads,), out_shape=(jax.ShapeDtypeStru...  13.8 us
    dot_general x1, matrix products, local(): lax.dot_general(gather_cot(out_cot), out_weight, NT, preferred_element_ty...  4.75 us
    transpose x1, local copies, waits for them, and re-layouts, local(): value_grad = vg.reshape(heads, rows, refl, width).transpose(1, 0, 2, 3)  3.22 us

profile of v1, /device:TPU:1, one launch (start us, length us, event | category | flops | bytes accessed | tf_op | source)
XLA Modules:
  0.0 117.1 jit_solution(10415000563217943013)
XLA Ops:
  0.6 1.6 %copy.26 = bf16[16,8,4,128]{3,1,2,0:T(8,128)(2,1)} copy(bf16[16,8,4,128]{3,2,1,0:T(4,128)(2,1)} %bitcast.28) | data formatting | bytes 262144
  2.2 0.8 copy.17
  3.1 0.8 reshape.34.lg_ref
  3.8 2.0 %copy.16 = bf16[4,128,4,128]{3,2,1,0:T(4,128)(2,1)} copy(bf16[4,128,4,128]{3,2,0,1:T(4,128)(2,1)} %bitcast.26) | data formatting | bytes 1048576 | tf_op jit(solution)/shard_map/transpose | solution.py:447
  5.8 2.1 %copy.18 = bf16[4,128,4,128]{3,2,1,0:T(4,128)(2,1)} copy(bf16[4,128,4,128]{3,2,0,1:T(4,128)(2,1)} %bitcast.27) | data formatting | bytes 1048576 | tf_op jit(solution)/shard_map/transpose | solution.py:448
  7.9 19.1 %gather_cot.1 = bf16[128,4096]{1,0:T(8,128)(2,1)} custom-call(bf16[128,1024]{1,0:T(8,128)(2,1)} %cot_ref.1), custom_call_target="tpu_custom_call" | custom-call | tf_op jit(solution)/shard_map/gather_cot/pallas_call | solution.py:84
  27.0 4.7 %fusion.g_ref = f32[128,512]{1,0:T(8,128)} fusion(bf16[128,4096]{1,0:T(8,128)(2,1)} %gather_cot.1, bf16[512,4096]{1,0:T(8,128)(2,1)} %param.11), kind=kOutput, calls=%fused_computation.3 | convolution fusion | flops 536870912 | bytes 5505024 | tf_op jit(solution)/shard_map/dot_general | solution.py:443
  31.8 29.2 %head_maps.1 = (f32[8,2,128,128]{3,2,1,0:T(8,128)}, f32[4,4,2,128,128]{4,3,2,1,0:T(8,128)}, f32[4,4,2,128,128]{4,3,2,1,0:T(8,128)}, f32[4,4,2,128,128]{4,3,2,1,0:T(8,128)}, f32[4,4,2,128,128]{4,3,2,1,0:T(8,128)}) custom-call(bf16[128,512]{1,0:T(8,128)(2,1)} %bitcast.21, bf16[4,512,128]{2,1,0:T(8,128)(2,1)} %bitcast.18, bf16[4,512,128]{2,1,0:T(8,128)(2,1)} %bitcast.20, ...), custom_call_target="tpu_custom_call" | custom-call | tf_op jit(solution)/shard_map/head_maps/pallas_call | solution.py:190
  60.9 36.5 %scan_states.1.ent_ref = f32[8,128,128]{2,1,0:T(8,128)} custom-call(f32[8,2,128,128]{3,2,1,0:T(8,128)} %get-tuple-element.13.maps_ref), custom_call_target="tpu_custom_call" | custom-call | tf_op jit(solution)/shard_map/scan_states/pallas_call | solution.py:335
  97.4 13.8 %head_grads.1 = (f32[128,512]{1,0:T(8,128)}, f32[4,512,128]{2,1,0:T(8,128)}, f32[4,512,128]{2,1,0:T(8,128)}, f32[4,4,128]{2,1,0:T(4,128)}) custom-call(bf16[128,512]{1,0:T(8,128)(2,1)} %bitcast.22, bf16[4,512,128]{2,1,0:T(8,128)(2,1)} %bitcast.19, f32[4,4,128]{2,1,0:T(4,128)} %reshape.34.lg_ref, f32[128,512]{1,0:T(8,128)} %fusion.g_ref, ...), custom_call_target="tpu_custom_call" | custom-call | tf_op jit(solution)/shard_map/head_grads/pallas_call | solution.py:411
  111.2 0.0 copy-start
  111.2 1.7 %reshape.36 = f32[128,4,128]{2,1,0:T(4,128)} reshape(f32[128,512]{1,0:T(8,128)} %get-tuple-element.18) | data formatting | bytes 524288 | tf_op jit(solution)/shard_map/reshape | solution.py:453
  112.9 3.2 %copy_bitcast_fusion = (f32[128,4,4,128]{3,2,1,0:T(4,128)}, f32[128,4,4,128]{3,2,1,0:T(4,128)}) fusion(f32[4,128,4,128]{3,2,1,0:T(4,128)} %bitcast.25, f32[4,128,4,128]{3,2,1,0:T(4,128)} %bitcast.24), kind=kLoop, calls=%fused_computation | loop fusion | bytes 4194304 | tf_op jit(solution)/shard_map/transpose | solution.py:455
  116.1 0.0 copy-done
  116.1 0.3 reshape.39
  116.4 0.7 copy.21
Async XLA Ops:
  111.2 5.0 %copy-start = (f32[4,4,128]{2,1,0:T(4,128)S(1)}, f32[4,4,128]{2,1,0:T(4,128)}, u32[]{:S(2)}) copy-start(f32[4,4,128]{2,1,0:T(4,128)} %get-tuple-element.21) | copy-start | bytes 24580

commit v2 on v0

v2 whole, which is shorter than its diff:
```python
import jax
import jax.numpy as jnp
from jax import lax
from jax.experimental import pallas as pl
from jax.experimental.pallas import tpu as pltpu
from jax.sharding import PartitionSpec as P

F32 = jnp.float32
BF16 = jnp.bfloat16
MESH = pl.DeviceIdType.MESH
HD = 128
BLK = 128
NT = (((1,), (1,)), ((), ()))
NN = (((1,), (0,)), ((), ()))


def dg(a, b, dims):
    return lax.dot_general(a, b, dims, preferred_element_type=F32)


def split(x):
    hi = x.astype(BF16)
    lo = (x - hi.astype(F32)).astype(BF16)
    return hi, lo


def dot2(a, bs):
    return dg(jnp.concatenate([a, a], 1), jnp.concatenate(bs, 0), NN)


def dot2l(as_, b):
    return dg(jnp.concatenate(as_, 1), jnp.concatenate([b, b], 0), NN)


def dot3(as_, bs):
    left = jnp.concatenate([as_[0], as_[1], as_[0]], 1)
    right = jnp.concatenate([bs[0], bs[0], bs[1]], 0)
    return dg(left, right, NN)


def dot3t(as_, bs):
    left = jnp.concatenate([as_[0], as_[1], as_[0]], 1)
    right = jnp.concatenate([bs[0], bs[0], bs[1]], 1)
    return dg(left, right, NT)


def iota2(shape, axis):
    return lax.broadcasted_iota(jnp.int32, shape, axis)


def to_row(full, eye):
    return jnp.sum(jnp.where(eye, full, 0.0), axis=0, keepdims=True)


def layer_kernel(q_ref, k_ref, v_ref, lg_ref, cot_ref, w_ref,
                 qg_ref, kg_ref, vg_ref, lgg_ref,
                 wide, kh, ktr, vh, qh, rsf, btf, invt, gsp, fa, fb, ba, bb,
                 full, wbuf, maps, rbuf, pref, total, entry_in, chain_out, entries, backs,
                 w_sem, cot_own, cot_send, cot_recv, send_sem, recv_sem, own_sem,
                 chain_send, chain_recv, back_send, back_recv):
    heads, refl, rows = lg_ref.shape
    steps = rows * refl
    count = steps // BLK
    tokens = rows // count
    scale = HD ** (-0.5)
    lanes = 2 * heads
    zsize = lax.axis_size("head")
    seq = lax.axis_size("seq")
    lines = seq // lanes
    zme = lax.axis_index("head")
    index = lax.axis_index("seq")
    line = index // lanes
    me = lax.rem(index, lanes)
    back = lax.rem(me, 2)
    home = me // 2
    base = line * lanes
    first = back * (lines - 1)
    last = (1 - back) * (lines - 1)
    ahead = lax.rem(line + 1 - 2 * back + lines, lines)
    behind = lax.rem(line - 1 + 2 * back + lines, lines)

    fetch_w = pltpu.make_async_copy(w_ref, wbuf, w_sem)
    fetch_w.start()
    barrier = pltpu.get_barrier_semaphore()
    for step in range(1, zsize):
        peer = lax.rem(zme + step, zsize)
        pl.semaphore_signal(barrier, inc=1, device_id={"head": peer}, device_id_type=MESH)
    for step in range(1, lanes):
        peer = base + lax.rem(me + step, lanes)
        pl.semaphore_signal(barrier, inc=1, device_id={"seq": peer}, device_id_type=MESH)
    for other in (ahead, behind):
        pl.semaphore_signal(
            barrier, inc=1, device_id={"seq": other * lanes + me}, device_id_type=MESH
        )

    per_token = heads * refl
    wide[...] = k_ref[...].astype(F32)
    for h in range(heads):
        for r in range(refl):
            kh[h, pl.ds(r, rows, stride=refl), :] = wide[
                pl.ds(h * refl + r, rows, stride=per_token), :
            ]
    wide[...] = v_ref[...].astype(F32)
    for h in range(heads):
        for r in range(refl):
            vh[h, pl.ds(r, rows, stride=refl), :] = wide[
                pl.ds(h * refl + r, rows, stride=per_token), :
            ]
    wide[pl.ds(0, rows * heads), :] = q_ref[...].astype(F32)
    for h in range(heads):
        qh[h] = wide[pl.ds(h, rows, stride=heads), :].astype(BF16)

    pl.semaphore_wait(barrier, zsize + lanes)

    cot_copies = []
    for step in range(1, zsize):
        copy = pltpu.make_async_remote_copy(
            src_ref=cot_ref,
            dst_ref=full.at[zme],
            send_sem=cot_send.at[step],
            recv_sem=cot_recv.at[step],
            device_id={"head": lax.rem(zme + step, zsize)},
            device_id_type=MESH,
        )
        copy.start()
        cot_copies.append(copy)
    own_cot = pltpu.make_async_copy(cot_ref, full.at[zme], cot_own)
    own_cot.start()

    row = iota2((BLK, BLK), 0)
    col = iota2((BLK, BLK), 1)
    eye = row == col
    eye_f = jnp.where(eye, 1.0, 0.0)
    zero = jnp.zeros((BLK, HD), F32)

    def level(s):
        same = (row // (2 * s)) == (col // (2 * s))
        return same & ((row // s) % 2 == 1) & ((col // s) % 2 == 0)

    def post(peer):
        @pl.when(peer != me)
        def post_other():
            pltpu.make_async_remote_copy(
                src_ref=maps.at[peer],
                dst_ref=rbuf.at[me],
                send_sem=send_sem.at[peer],
                recv_sem=recv_sem.at[me],
                device_id={"seq": base + peer},
                device_id_type=MESH,
            ).start()

        @pl.when(peer == me)
        def post_own():
            pltpu.make_async_copy(maps.at[peer], rbuf.at[peer], own_sem).start()

    def forward(turn, carry):
        pair = (lax.rem(home + 2 + turn, heads), lax.rem(home + 1 - turn, heads))
        units = [(h, b) for b in range(count) for h in pair]
        lower, inv = [], []
        for h, b in units:
            span = pl.ds(b * BLK, BLK)
            kf = kh[h, span, :]
            kb = kf.astype(BF16)
            rs = lax.rsqrt(jnp.sum(kf * kf, axis=1, keepdims=True) + 1e-06)
            beta4 = 2.0 / (1.0 + jnp.exp(-lg_ref[h]))
            beta_all = jnp.tile(jnp.concatenate([beta4] * (8 // refl), 0), (BLK // 8, 1))
            beta = jnp.sum(
                jnp.where(col == row // refl + b * tokens, beta_all, 0.0), axis=1, keepdims=True
            )
            rs = jnp.broadcast_to(rs, (BLK, HD))
            beta = jnp.broadcast_to(beta, (BLK, HD))
            rsf[h, span, :] = rs
            btf[h, span, :] = beta
            ktr[h, b] = kb.T
            n = jnp.where(col < row, dg(kb, kb, NT) * (rs * beta) * to_row(rs, eye), 0.0)
            lower.append(n)
        mask = level(1)
        for n in lower:
            inv.append(eye_f - jnp.where(mask, n, 0.0))
        s = 2
        while s < BLK:
            mask = level(s)
            for i, n in enumerate(lower):
                xs = split(inv[i])
                y = dot3(xs, split(jnp.where(mask, n, 0.0)))
                inv[i] = inv[i] - dot3(split(y), xs)
            s *= 2
        invs = [split(x) for x in inv]
        for (h, b), x in zip(units, invs):
            invt[h, b, 0] = x[0].T
            invt[h, b, 1] = x[1].T
        state = [jnp.concatenate([eye_f, zero], axis=1) for h in pair]
        for b in range(count):
            span = pl.ds(b * BLK, BLK)
            for i, h in enumerate(pair):
                now = state[i]
                kb = kh[h, span, :].astype(BF16)
                rs = rsf[h, span, :]
                beta = btf[h, span, :]
                moved = dot2(kb, split(now))
                y = jnp.concatenate(
                    [(-rs * beta) * moved[:, :HD], beta * (vh[h, span, :] - rs * moved[:, HD:])],
                    axis=1,
                )
                d = dot3(invs[b * len(pair) + i], split(y))
                fa[h, b, 0] = now[:, :HD]
                fb[h, b, 0] = now[:, HD:]
                fa[h, b, 1] = d[:, :HD]
                fb[h, b, 1] = d[:, HD:]
                rs2 = jnp.concatenate([rs, rs], axis=1)
                state[i] = now + dot2(ktr[h, b], split(rs2 * d))
        for i, h in enumerate(pair):
            maps[2 * h, 0] = state[i][:, :HD]
            maps[2 * h, 1] = state[i][:, HD:]
        for h in pair:
            post(2 * h)
        return carry

    lax.fori_loop(0, heads // 2, forward, 0)

    own_cot.wait()
    for copy in cot_copies:
        copy.wait()
    fetch_w.wait()
    width = cot_ref.shape[1]
    for n in range(heads // 2):
        acc = jnp.zeros((rows, 2 * HD), F32)
        for j in range(zsize):
            acc = acc + dg(
                full[j],
                wbuf[2 * n * HD : 2 * (n + 1) * HD, j * width : (j + 1) * width],
                NT,
            )
        for i in range(2):
            hi, lo = split(acc[:, i * HD : (i + 1) * HD])
            gsp[2 * n + i, 0] = hi
            gsp[2 * n + i, 1] = lo

    seen_t = (iota2((BLK, tokens), 0) // refl) <= iota2((BLK, tokens), 1)

    def backward(turn, carry):
        pair = (lax.rem(home + 2 + turn, heads), lax.rem(home + 1 - turn, heads))
        state = [jnp.concatenate([eye_f, zero], axis=1) for h in pair]
        for b in reversed(range(count)):
            span = pl.ds(b * BLK, BLK)
            tspan = pl.ds(b * tokens, tokens)
            for i, h in enumerate(pair):
                now = state[i]
                kb = kh[h, span, :].astype(BF16)
                rs = rsf[h, span, :]
                beta = btf[h, span, :]
                qb = qh[h, tspan, :]
                gs = (gsp[h, 0, tspan, :], gsp[h, 1, tspan, :])
                sc_t = jnp.where(seen_t, dg(kb, qb, NT) * (rs[:, :tokens] * scale), 0.0)
                direct = dot3(split(sc_t), gs)
                moved = dot2(kb, split(now))
                dd = jnp.concatenate([rs * moved[:, :HD], rs * moved[:, HD:] + direct], axis=1)
                f = dot3((invt[h, b, 0], invt[h, b, 1]), split(dd))
                ba[h, b, 0] = now[:, :HD]
                bb[h, b, 0] = now[:, HD:]
                ba[h, b, 1] = f[:, :HD]
                bb[h, b, 1] = f[:, HD:]
                source = dot2(qb.T, gs) * scale
                rb = rs * beta
                rb2 = jnp.concatenate([rb, rb], axis=1)
                state[i] = (
                    now
                    + jnp.concatenate([zero, source], axis=1)
                    - dot2(ktr[h, b], split(rb2 * f))
                )
        for i, h in enumerate(pair):
            maps[2 * h + 1, 0] = state[i][:, :HD]
            maps[2 * h + 1, 1] = state[i][:, HD:]
        for h in pair:
            post(2 * h + 1)
        return carry

    lax.fori_loop(0, heads // 2, backward, 0)

    total[:, :HD] = eye_f
    total[:, HD:] = zero

    def advance(step, carry):
        source = step + back * (lanes - 1 - 2 * step)

        @pl.when(source == me)
        def wait_own():
            pltpu.make_async_copy(maps.at[me], rbuf.at[me], own_sem).wait()

        @pl.when(source != me)
        def wait_other():
            pltpu.make_async_remote_copy(
                src_ref=maps.at[source],
                dst_ref=rbuf.at[source],
                send_sem=send_sem.at[source],
                recv_sem=recv_sem.at[source],
                device_id={"seq": base + source},
                device_id_type=MESH,
            ).wait_recv()

        now = total[...]
        pref[source] = now
        moved = dot3(split(rbuf[source, 0]), split(now))
        total[:, :HD] = moved[:, :HD]
        total[:, HD:] = moved[:, HD:] + rbuf[source, 1]
        return carry

    lax.fori_loop(0, lanes, advance, 0)

    chain = pltpu.make_async_remote_copy(
        src_ref=chain_out,
        dst_ref=entry_in,
        send_sem=chain_send,
        recv_sem=chain_recv,
        device_id={"seq": ahead * lanes + me},
        device_id_type=MESH,
    )

    @pl.when(line == first)
    def start_zero():
        entry_in[...] = jnp.zeros((HD, HD), F32)

    @pl.when(line != first)
    def start_chain():
        chain.wait_recv()

    states = split(entry_in[...])

    @pl.when(line != last)
    def pass_on():
        chain_out[...] = dot3(split(total[:, :HD]), states) + total[:, HD:]
        chain.start()

    def give(peer):
        return pltpu.make_async_remote_copy(
            src_ref=entries.at[peer],
            dst_ref=backs.at[me],
            send_sem=back_send.at[peer],
            recv_sem=back_recv.at[me],
            device_id={"seq": base + peer},
            device_id_type=MESH,
        )

    def finish(step, carry):
        peer = lax.rem(me + step, lanes)
        entries[peer] = dot3(split(pref[peer, :, :HD]), states) + pref[peer, :, HD:]
        give(peer).start()
        return carry

    lax.fori_loop(1, lanes, finish, 0)
    backs[me] = dot3(split(pref[me, :, :HD]), states) + pref[me, :, HD:]

    seen = (iota2((tokens, BLK), 1) // refl) <= iota2((tokens, BLK), 0)

    def take(source):
        @pl.when(source != me)
        def take_other():
            pltpu.make_async_remote_copy(
                src_ref=entries.at[source],
                dst_ref=backs.at[source],
                send_sem=back_send.at[source],
                recv_sem=back_recv.at[source],
                device_id={"seq": base + source},
                device_id_type=MESH,
            ).wait_recv()

    def grads(turn, carry):
        offset = turn + (turn // 2) * (1 - 2 * lax.rem(turn, 2))
        h = lax.rem(home + offset, heads)
        take(2 * h)
        take(2 * h + 1)
        begin = split(backs[2 * h])
        final = split(backs[2 * h + 1])
        acc = jnp.zeros((8, rows), F32)
        for b in range(count):
            span = pl.ds(b * BLK, BLK)
            tspan = pl.ds(b * tokens, tokens)
            kf = kh[h, span, :]
            kb = kf.astype(BF16)
            rs = rsf[h, span, :]
            beta = btf[h, span, :]
            rs_row = to_row(rs, eye)
            s0 = dot3(split(fa[h, b, 0]), begin) + fb[h, b, 0]
            delta = dot3(split(fa[h, b, 1]), begin) + fb[h, b, 1]
            lam = dot3(split(ba[h, b, 0]), final) + bb[h, b, 0]
            f = dot3(split(ba[h, b, 1]), final) + bb[h, b, 1]
            e = beta * f
            dlog = jnp.sum(f * delta, axis=1, keepdims=True) * (1.0 - 0.5 * beta)
            dlog = jnp.where(col == row // refl + b * tokens, dlog, 0.0)
            for i in range(BLK // 8):
                acc = acc + dlog[8 * i : 8 * (i + 1), :]
            vg_ref[h, span, :] = e
            qb = qh[h, tspan, :]
            gs = (gsp[h, 0, tspan, :], gsp[h, 1, tspan, :])
            ds, es, ss, ls = split(delta), split(e), split(s0), split(lam)
            dsc = jnp.where(seen, dot3t(gs, ds), 0.0)
            qg_ref[h, tspan, :] = scale * (dot3t(gs, ss) + dot2l(split(dsc * rs_row), kb))
            m = jnp.where(col < row, dot3t(es, ds), 0.0)
            sym = (m + m.T) * rs_row
            dk = (
                dot3t(ds, ls)
                - dot3t(es, ss)
                + dot2l(split(dsc.T * scale), qb)
                - dot2l(split(sym), kb)
            )
            ku = kf * rs
            along = jnp.sum(ku * dk, axis=1, keepdims=True)
            kg_ref[h, span, :] = rs * (dk - ku * along)
        out = acc[:refl]
        for i in range(1, 8 // refl):
            out = out + acc[i * refl : (i + 1) * refl]
        lgg_ref[h] = out
        return carry

    lax.fori_loop(0, heads, grads, 0)

    def drain(step, carry):
        peer = lax.rem(me + step, lanes)
        pltpu.make_async_remote_copy(
            src_ref=maps.at[peer],
            dst_ref=rbuf.at[me],
            send_sem=send_sem.at[peer],
            recv_sem=recv_sem.at[me],
            device_id={"seq": base + peer},
            device_id_type=MESH,
        ).wait_send()
        give(peer).wait_send()
        return carry

    lax.fori_loop(1, lanes, drain, 0)

    @pl.when(line != last)
    def sent_on():
        chain.wait_send()


def layer(q, k, v, lg, cot, w):
    heads, refl, rows = lg.shape
    steps = rows * refl
    count = steps // BLK
    lanes = 2 * heads
    zsize = lax.axis_size("head")
    dma = pltpu.SemaphoreType.DMA
    vm = pl.BlockSpec(memory_space=pltpu.VMEM)
    saved = pltpu.VMEM((heads, count, 2, BLK, HD), F32)
    return pl.pallas_call(
        layer_kernel,
        out_shape=(
            jax.ShapeDtypeStruct((heads, rows, HD), F32),
            jax.ShapeDtypeStruct((heads, steps, HD), F32),
            jax.ShapeDtypeStruct((heads, steps, HD), F32),
            jax.ShapeDtypeStruct(lg.shape, F32),
        ),
        in_specs=[vm] * 5 + [pl.BlockSpec(memory_space=pl.ANY)],
        out_specs=(vm,) * 4,
        scratch_shapes=[
            pltpu.VMEM((rows * heads * refl, HD), F32),
            pltpu.VMEM((heads, steps, HD), F32),
            pltpu.VMEM((heads, count, HD, BLK), BF16),
            pltpu.VMEM((heads, steps, HD), F32),
            pltpu.VMEM((heads, rows, HD), BF16),
            pltpu.VMEM((heads, steps, HD), F32),
            pltpu.VMEM((heads, steps, HD), F32),
            pltpu.VMEM((heads, count, 2, BLK, BLK), BF16),
            pltpu.VMEM((heads, 2, rows, HD), BF16),
            saved, saved, saved, saved,
            pltpu.VMEM((zsize,) + cot.shape, BF16),
            pltpu.VMEM(w.shape, BF16),
            pltpu.VMEM((lanes, 2, HD, HD), F32),
            pltpu.VMEM((lanes, 2, HD, HD), F32),
            pltpu.VMEM((lanes, HD, 2 * HD), F32),
            pltpu.VMEM((HD, 2 * HD), F32),
            pltpu.VMEM((HD, HD), F32),
            pltpu.VMEM((HD, HD), F32),
            pltpu.VMEM((lanes, HD, HD), F32),
            pltpu.VMEM((lanes, HD, HD), F32),
            dma, dma, dma((zsize,)), dma((zsize,)),
            dma((lanes,)), dma((lanes,)), dma,
            dma, dma, dma((lanes,)), dma((lanes,)),
        ],
        compiler_params=pltpu.CompilerParams(collective_id=0, has_side_effects=True),
        name="layer",
    )(q, k, v, lg, cot, w)


def local(queries, keys, values, beta_logits, out_cot, out_weight):
    rows, heads, width = queries.shape
    refl = keys.shape[2]
    qg, kg, vg, lgg = layer(
        queries.reshape(rows * heads, width),
        keys.reshape(rows * heads * refl, width),
        values.reshape(rows * heads * refl, width),
        beta_logits,
        out_cot,
        out_weight,
    )
    query_grad = qg.transpose(1, 0, 2)
    key_grad = kg.reshape(heads, rows, refl, width).transpose(1, 0, 2, 3)
    value_grad = vg.reshape(heads, rows, refl, width).transpose(1, 0, 2, 3)
    return (query_grad, key_grad, value_grad, lgg)


def solution(mesh):
    return jax.shard_map(
        local,
        mesh=mesh,
        in_specs=(
            P("seq", "head", None),
            P("seq", "head", None, None),
            P("seq", "head", None, None),
            P("head", None, "seq"),
            P("seq", "head"),
            P("head", None),
        ),
        out_specs=(
            P("seq", "head", None),
            P("seq", "head", None, None),
            P("seq", "head", None, None),
            P("head", None, "seq"),
        ),
        check_vma=False,
    )
```

time: 851 us -> 76.1 us (0.09); the launches traced: 837 us -> 75.9 us
  matrix products: 249 us -> 0 us
  waiting for transfers between devices: 212 us -> 0 us
  other arithmetic: 163 us -> 0 us
  starting transfers between devices: 156 us -> 0 us
  Pallas kernels: 0 us -> 69.6 us
  local copies, waits for them, and re-layouts: 40 us -> 5.65 us
  between operations: 14.8 us -> 0.65 us
    dot_general x108 -> x0, matrix products: 238 us -> none  [the longest x106 231 us: product(): return jnp.matmul(left, right, precision=precise)]
    ppermute x62 -> x0, waiting for transfers between devices: 211 us -> none  [shifted(): lax.ppermute(value, axis, [(source, source + steps) for source in range(l...]
    another operation x4 -> x0, other arithmetic: 159 us -> none  [block_maps(): jax.scipy.linalg.solve_triangular(system, right_side, lower=True, unit_di...]
    ppermute x62 -> x0, starting transfers between devices: 156 us -> none  [shifted(): lax.ppermute(value, axis, [(source, source + steps) for source in range(l...]
    pallas_call x0 -> x1, Pallas kernels: none -> 69.6 us  [layer(): pl.pallas_call(layer_kernel, out_shape=(jax.ShapeDtypeStruct((heads, rows...]
    while x24 -> x0, local copies, waits for them, and re-layouts: 15.4 us -> none
    another operation x3 -> x0, matrix products: 10.8 us -> none  [block_maps(): jax.scipy.linalg.solve_triangular(system, right_side, lower=True, unit_di...]
  transfers between devices with their start and end apart: 63 -> 0, of which waited for: 31 -> 0; matrix products, arithmetic and copies ran while one was open for 32% -> 0% of each run, Pallas kernels for 0% -> 0%
where the time goes in v2:
time: 76.1 us; the launch traced here: 75.9 us
  Pallas kernels  69.6 us (91%)
  local copies, waits for them, and re-layouts  5.65 us (7%)
    pallas_call x1, Pallas kernels, layer(): pl.pallas_call(layer_kernel, out_shape=(jax.ShapeDtypeStruct((heads, rows...  69.6 us
    transpose x1, local copies, waits for them, and re-layouts, local(): value_grad = vg.reshape(heads, rows, refl, width).transpose(1, 0, 2, 3)  3.22 us
    unnamed x4, local copies, waits for them, and re-layouts  2.43 us

profile of v2, /device:TPU:1, one launch (start us, length us, event | category | flops | bytes accessed | tf_op | source)
XLA Modules:
  0.0 75.9 jit_solution(12609001285513474823)
XLA Ops:
  0.6 69.6 %layer.1 = (f32[4,128,128]{2,1,0:T(8,128)}, f32[4,512,128]{2,1,0:T(8,128)}, f32[4,512,128]{2,1,0:T(8,128)}, f32[4,4,128]{2,1,0:T(4,128)}) custom-call(bf16[512,128]{1,0:T(8,128)(2,1)} %bitcast.15, bf16[2048,128]{1,0:T(8,128)(2,1)} %bitcast.12, bf16[2048,128]{1,0:T(8,128)(2,1)} %bitcast.13, f32[4,4,128]{2,1,0:T(4,128)} %lg_ref.1, bf16[128,1024]{1,0:T(8,128)(2,1)} %cot_ref.1, ...), custom_call_target="tpu_custom_call" | custom-call | tf_op jit(solution)/shard_map/layer/pallas_call | solution.py:446
  70.2 0.0 copy-start
  70.2 1.8 %copy.12 = f32[128,4,128]{2,1,0:T(4,128)} copy(f32[128,4,128]{2,0,1:T(8,128)} %bitcast.14) | data formatting | bytes 524288
  72.1 3.2 %copy_bitcast_fusion = (f32[128,4,4,128]{3,2,1,0:T(4,128)}, f32[128,4,4,128]{3,2,1,0:T(4,128)}) fusion(f32[4,128,4,128]{3,2,1,0:T(4,128)} %bitcast.11, f32[4,128,4,128]{3,2,1,0:T(4,128)} %bitcast.10), kind=kLoop, calls=%fused_computation | loop fusion | bytes 4194304 | tf_op jit(solution)/shard_map/transpose | solution.py:499
  75.3 0.0 copy-done
  75.3 0.6 copy.16
Async XLA Ops:
  70.2 5.1 %copy-start = (f32[4,4,128]{2,1,0:T(4,128)S(1)}, f32[4,4,128]{2,1,0:T(4,128)}, u32[]{:S(2)}) copy-start(f32[4,4,128]{2,1,0:T(4,128)} %get-tuple-element.25) | copy-start | bytes 24580

commit v3 on v2

v3 whole, which is shorter than its diff:
```python
import jax
import jax.numpy as jnp
from jax import lax
from jax.experimental import pallas as pl
from jax.experimental.pallas import tpu as pltpu
from jax.sharding import PartitionSpec as P

F32 = jnp.float32
BF16 = jnp.bfloat16
MESH = pl.DeviceIdType.MESH
HD = 128
BLK = 128
NT = (((1,), (1,)), ((), ()))
NN = (((1,), (0,)), ((), ()))


def dg(a, b, dims):
    return lax.dot_general(a, b, dims, preferred_element_type=F32)


def split(x):
    hi = x.astype(BF16)
    lo = (x - hi.astype(F32)).astype(BF16)
    return hi, lo


def dot2(a, bs):
    return dg(jnp.concatenate([a, a], 1), jnp.concatenate(bs, 0), NN)


def dot2l(as_, b):
    return dg(jnp.concatenate(as_, 1), jnp.concatenate([b, b], 0), NN)


def dot3(as_, bs):
    left = jnp.concatenate([as_[0], as_[1], as_[0]], 1)
    right = jnp.concatenate([bs[0], bs[0], bs[1]], 0)
    return dg(left, right, NN)


def dot3t(as_, bs):
    left = jnp.concatenate([as_[0], as_[1], as_[0]], 1)
    right = jnp.concatenate([bs[0], bs[0], bs[1]], 1)
    return dg(left, right, NT)


def iota2(shape, axis):
    return lax.broadcasted_iota(jnp.int32, shape, axis)


def to_row(full, eye):
    return jnp.sum(jnp.where(eye, full, 0.0), axis=0, keepdims=True)


def remote(src, dst, send, recv, **device):
    return pltpu.make_async_remote_copy(
        src_ref=src,
        dst_ref=dst,
        send_sem=send,
        recv_sem=recv,
        device_id=device,
        device_id_type=MESH,
    )


def diagonal_inverse(lower, small, row, col, spread):
    units = len(lower)
    packed = []
    band = col[:small] // small
    for n in lower:
        acc = jnp.where(band == 0, n[:small], 0.0)
        for i in range(1, BLK // small):
            acc = jnp.where(band == i, n[i * small : (i + 1) * small], acc)
        packed.append(acc)
    hi, lo = split(jnp.concatenate(packed, 0))
    both = jnp.concatenate([hi, lo], 1)
    unit = jnp.where(row[:small] == col[:small] % small, 1.0, 0.0)
    xs = [unit] * units
    for j in range(small - 1):
        factor = dg(both, spread[j], NN)
        for u in range(units):
            xs[u] = xs[u] - factor[u * small : (u + 1) * small] * xs[u][j : j + 1]
    return [
        jnp.concatenate([jnp.where(band == i, x, 0.0) for i in range(BLK // small)], 0)
        for x in xs
    ]


def grow_inverse(inv, lower, s, row, col):
    mask = ((row // (2 * s)) == (col // (2 * s))) & ((col // s) % 2 == 0)
    odds = [slice(i, i + s) for i in range(s, BLK, 2 * s)]
    grown = []
    for x, n in zip(inv, lower):
        cut = jnp.where(mask, n, 0.0)
        below = jnp.concatenate([cut[o] for o in odds], 0)
        y = dot3(split(below), split(x))
        gap = jnp.zeros((s, BLK), F32)
        parts = []
        for i in range(len(odds)):
            parts += [gap, y[i * s : (i + 1) * s]]
        odd = jnp.concatenate([x[o] for o in odds], 0)
        new = odd - dot3(split(odd), split(jnp.concatenate(parts, 0)))
        parts = []
        for i, o in enumerate(odds):
            parts += [x[o.start - s : o.start], new[i * s : (i + 1) * s]]
        grown.append(jnp.concatenate(parts, 0))
    return grown


def layer_kernel(q_ref, k_ref, v_ref, lg_ref, cot_ref, w_ref,
                 qg_ref, kg_ref, vg_ref, lgg_ref,
                 wide, kh, ktr, vh, qh, rsf, btf, invn, invt, gsp, fa, fb, ba, bb,
                 full, wbuf, mine, pm, comp, rbuf, pref, total, entry_in, ahead_map, chain_out,
                 entries, both,
                 w_sem, cot_own, cot_send, cot_recv, pm_send, pm_recv, comp_send, comp_recv,
                 chain_send, chain_recv, map_recv, ent_send, ent_recv, oth_send, oth_recv):
    heads, refl, rows = lg_ref.shape
    steps = rows * refl
    count = steps // BLK
    tokens = rows // count
    scale = HD ** (-0.5)
    lanes = 2 * heads
    zsize = lax.axis_size("head")
    lines = lax.axis_size("seq") // lanes
    zme = lax.axis_index("head")
    index = lax.axis_index("seq")
    line = index // lanes
    me = lax.rem(index, lanes)
    back = lax.rem(me, 2)
    home = me // 2
    partner = index + 1 - 2 * back
    rank = line + back * (lines - 1 - 2 * line)

    def chip(x):
        return line * lanes + 2 * x + back

    def at_rank(r):
        return (r + back * (lines - 1 - 2 * r)) * lanes + me

    fetch_w = pltpu.make_async_copy(w_ref, wbuf, w_sem)
    fetch_w.start()
    barrier = pltpu.get_barrier_semaphore()
    zright = lax.rem(zme + 1, zsize)
    zleft = lax.rem(zme + zsize - 1, zsize)
    for peer in (zright, zleft):
        pl.semaphore_signal(barrier, inc=1, device_id={"head": peer}, device_id_type=MESH)
    friends = [partner]
    friends += [chip(lax.rem(home + step, heads)) for step in range(1, heads)]
    friends += [lax.rem(line + step, lines) * lanes + me for step in range(1, lines)]
    for peer in friends:
        pl.semaphore_signal(barrier, inc=1, device_id={"seq": peer}, device_id_type=MESH)

    per_token = heads * refl
    wide[...] = k_ref[...].astype(F32)
    for h in range(heads):
        for r in range(refl):
            kh[h, pl.ds(r, rows, stride=refl), :] = wide[
                pl.ds(h * refl + r, rows, stride=per_token), :
            ]

    half = rows // 2
    low, high = pl.ds(0, half), pl.ds(half, half)
    cot_copies = [
        remote(cot_ref.at[low], full.at[zme, low], cot_send.at[0], cot_recv.at[0], head=zright),
        remote(cot_ref.at[high], full.at[zme, high], cot_send.at[1], cot_recv.at[1], head=zleft),
        remote(cot_ref.at[high], full.at[zme, high], cot_send.at[2], cot_recv.at[2], head=zright),
        remote(cot_ref.at[low], full.at[zme, low], cot_send.at[3], cot_recv.at[3], head=zleft),
    ]
    own_cot = pltpu.make_async_copy(cot_ref, full.at[zme], cot_own)
    own_cot.start()
    hand_right = remote(
        full.at[zleft, low], full.at[zleft, low], cot_send.at[4], cot_recv.at[4], head=zright
    )
    hand_left = remote(
        full.at[zright, high], full.at[zright, high], cot_send.at[5], cot_recv.at[5], head=zleft
    )

    wide[...] = v_ref[...].astype(F32)
    for h in range(heads):
        for r in range(refl):
            vh[h, pl.ds(r, rows, stride=refl), :] = wide[
                pl.ds(h * refl + r, rows, stride=per_token), :
            ]
    wide[pl.ds(0, rows * heads), :] = q_ref[...].astype(F32)
    for h in range(heads):
        qh[h] = wide[pl.ds(h, rows, stride=heads), :].astype(BF16)

    row = iota2((BLK, BLK), 0)
    col = iota2((BLK, BLK), 1)
    eye = row == col
    eye_f = jnp.where(eye, 1.0, 0.0)
    zero = jnp.zeros((BLK, HD), F32)
    small = 16

    def invert(turn, carry):
        @pl.when(turn == 1)
        def greet():
            pl.semaphore_wait(barrier, 2 + len(friends))
            for copy in cot_copies:
                copy.start()

        units = [(2 * turn + i, b) for b in range(count) for i in range(2)]
        lower = []
        for h, b in units:
            span = pl.ds(b * BLK, BLK)
            kf = kh[h, span, :]
            kb = kf.astype(BF16)
            rs = lax.rsqrt(jnp.sum(kf * kf, axis=1, keepdims=True) + 1e-06)
            beta4 = 2.0 / (1.0 + jnp.exp(-lg_ref[h]))
            beta_all = jnp.tile(jnp.concatenate([beta4] * (8 // refl), 0), (BLK // 8, 1))
            beta = jnp.sum(
                jnp.where(col == row // refl + b * tokens, beta_all, 0.0), axis=1, keepdims=True
            )
            rs = jnp.broadcast_to(rs, (BLK, HD))
            beta = jnp.broadcast_to(beta, (BLK, HD))
            rsf[h, span, :] = rs
            btf[h, span, :] = beta
            ktr[h, b] = kb.T
            n = jnp.where(col < row, dg(kb, kb, NT) * (rs * beta) * to_row(rs, eye), 0.0)
            lower.append(n)
        spread = []
        for j in range(small - 1):
            pick = jnp.where(row == (col // small) * small + j, 1.0, 0.0).astype(BF16)
            spread.append(jnp.concatenate([pick, pick], 0))
        inv = diagonal_inverse(lower, small, row, col, spread)
        s = small
        while s < BLK:
            inv = grow_inverse(inv, lower, s, row, col)
            s *= 2
        for (h, b), x in zip(units, inv):
            hi, lo = split(x)
            invn[h, b, 0] = hi
            invn[h, b, 1] = lo
            invt[h, b, 0] = hi.T
            invt[h, b, 1] = lo.T
        return carry

    lax.fori_loop(0, heads // 2, invert, 0)
    cot_copies[0].wait_recv()
    hand_right.start()
    cot_copies[1].wait_recv()
    hand_left.start()

    def hand_over(direction, h):
        return remote(mine.at[direction, h], pm.at[h], pm_send.at[h], pm_recv.at[h], seq=partner)

    def post(h):
        return remote(
            comp.at[h], rbuf.at[home], comp_send.at[h], comp_recv.at[home], seq=chip(h)
        )

    def combine(direction, h):
        hand_over(direction, h).wait_recv()
        moved = dot3(split(pm[h, :, :HD]), split(mine[direction, h]))
        moved = jnp.concatenate([moved[:, :HD], moved[:, HD:] + pm[h, :, HD:]], axis=1)

        @pl.when(h == home)
        def keep():
            rbuf[home] = moved

        @pl.when(h != home)
        def send():
            comp[h] = moved
            post(h).start()

    state = [jnp.concatenate([eye_f, zero], axis=1) for h in range(heads)]
    for b in range(count):
        span = pl.ds(b * BLK, BLK)
        for h in range(heads):
            now = state[h]
            kb = kh[h, span, :].astype(BF16)
            rs = rsf[h, span, :]
            beta = btf[h, span, :]
            moved = dot2(kb, split(now))
            y = jnp.concatenate(
                [(-rs * beta) * moved[:, :HD], beta * (vh[h, span, :] - rs * moved[:, HD:])],
                axis=1,
            )
            d = dot3((invn[h, b, 0], invn[h, b, 1]), split(y))
            fa[h, 2 * b] = now[:, :HD]
            fb[h, 2 * b] = now[:, HD:]
            fa[h, 2 * b + 1] = d[:, :HD]
            fb[h, 2 * b + 1] = d[:, HD:]
            rs2 = jnp.concatenate([rs, rs], axis=1)
            state[h] = now + dot2(ktr[h, b], split(rs2 * d))
    for h in range(heads):
        mine[0, h] = state[h]

    @pl.when(back == 1)
    def hand_forward():
        for h in range(heads):
            hand_over(0, h).start()

    own_cot.wait()
    cot_copies[2].wait_recv()
    cot_copies[3].wait_recv()
    hand_right.wait_recv()
    hand_left.wait_recv()
    fetch_w.wait()
    width = cot_ref.shape[1]
    for n in range(heads // 2):
        acc = jnp.zeros((rows, 2 * HD), F32)
        for j in range(zsize):
            acc = acc + dg(
                full[j],
                wbuf[2 * n * HD : 2 * (n + 1) * HD, j * width : (j + 1) * width],
                NT,
            )
        for i in range(2):
            hi, lo = split(acc[:, i * HD : (i + 1) * HD])
            gsp[2 * n + i, 0] = hi
            gsp[2 * n + i, 1] = lo

    def pair_of(turn):
        return (lax.rem(home + 2 + turn, heads), lax.rem(home + 1 - turn + heads, heads))

    @pl.when(back == 0)
    def combine_forward():
        for turn in range(heads // 2):
            for h in pair_of(turn):
                combine(0, h)

    seen_t = (iota2((BLK, tokens), 0) // refl) <= iota2((BLK, tokens), 1)

    def backward(turn, carry):
        pair = pair_of(turn)
        state = [jnp.concatenate([eye_f, zero], axis=1) for h in pair]
        for b in reversed(range(count)):
            span = pl.ds(b * BLK, BLK)
            tspan = pl.ds(b * tokens, tokens)
            for i, h in enumerate(pair):
                now = state[i]
                kb = kh[h, span, :].astype(BF16)
                rs = rsf[h, span, :]
                beta = btf[h, span, :]
                qb = qh[h, tspan, :]
                gs = (gsp[h, 0, tspan, :], gsp[h, 1, tspan, :])
                sc_t = jnp.where(seen_t, dg(kb, qb, NT) * (rs[:, :tokens] * scale), 0.0)
                direct = dot3(split(sc_t), gs)
                moved = dot2(kb, split(now))
                dd = jnp.concatenate([rs * moved[:, :HD], rs * moved[:, HD:] + direct], axis=1)
                f = dot3((invt[h, b, 0], invt[h, b, 1]), split(dd))
                ba[h, 2 * b] = now[:, :HD]
                bb[h, 2 * b] = now[:, HD:]
                ba[h, 2 * b + 1] = f[:, :HD]
                bb[h, 2 * b + 1] = f[:, HD:]
                source = dot2(qb.T, gs) * scale
                rb = rs * beta
                rb2 = jnp.concatenate([rb, rb], axis=1)
                state[i] = (
                    now
                    + jnp.concatenate([zero, source], axis=1)
                    - dot2(ktr[h, b], split(rb2 * f))
                )
        for i, h in enumerate(pair):
            mine[1, h] = state[i]

        @pl.when(back == 0)
        def hand_backward():
            for h in pair:
                hand_over(1, h).start()

        @pl.when((back == 1) & (turn == 1))
        def combine_backward():
            for h in pair_of(0):
                combine(1, h)

        return carry

    lax.fori_loop(0, heads // 2, backward, 0)

    @pl.when(back == 1)
    def combine_last():
        for h in pair_of(1):
            combine(1, h)

    total[:, :HD] = eye_f
    total[:, HD:] = zero

    def advance(step, carry):
        source = step + back * (heads - 1 - 2 * step)

        @pl.when(source != home)
        def wait_other():
            remote(
                comp.at[source], rbuf.at[source], comp_send.at[source], comp_recv.at[source],
                seq=chip(source),
            ).wait_recv()

        now = total[...]
        pref[source] = now
        moved = dot3(split(rbuf[source, :, :HD]), split(now))
        total[:, :HD] = moved[:, :HD]
        total[:, HD:] = moved[:, HD:] + rbuf[source, :, HD:]
        return carry

    lax.fori_loop(0, heads, advance, 0)

    def chain(r, slot):
        return remote(chain_out, entry_in, chain_send.at[slot], chain_recv, seq=at_rank(r))

    def chain_map():
        return remote(total, ahead_map, chain_send.at[0], map_recv, seq=at_rank(3))

    @pl.when(rank == 0)
    def begin_chain():
        chain_out[...] = total[:, HD:]
        chain(1, 0).start()
        entry_in[...] = zero

    @pl.when(rank == 2)
    def offer_map():
        chain_map().start()

    seen = (iota2((tokens, BLK), 1) // refl) <= iota2((tokens, BLK), 0)

    def visit(turn):
        return lax.rem(home + turn + (turn // 2) * (1 - 2 * lax.rem(turn, 2)), heads)

    def give(x):
        return remote(
            entries.at[x], both.at[back, home], ent_send.at[x], ent_recv.at[home], seq=chip(x)
        )

    def tell(h):
        return remote(
            entries.at[heads + h], both.at[back, h], oth_send.at[h], oth_recv.at[h], seq=partner
        )

    def told(h):
        remote(
            entries.at[heads + h], both.at[1 - back, h], oth_send.at[h], oth_recv.at[h],
            seq=partner,
        ).wait_recv()

    def relay(turn):
        h = visit(turn)

        @pl.when(h != home)
        def take():
            remote(
                entries.at[h], both.at[back, h], ent_send.at[h], ent_recv.at[h], seq=chip(h)
            ).wait_recv()

        entries[heads + h] = (
            dot3(split(mine[back, h, :, :HD]), split(both[back, h])) + mine[back, h, :, HD:]
        )
        tell(h).start()

    deep = 2 * count * BLK

    def first_part(turn, carry):
        h = visit(turn)

        @pl.when((back == 0) & (turn + 1 < heads))
        def look_ahead():
            relay(turn + 1)

        @pl.when(back == 1)
        def listen():
            told(h)

        begin = split(both[0, h])
        sd = dot3(split(fa[h].reshape(deep, HD)), begin) + fb[h].reshape(deep, HD)
        fb[h] = sd.reshape(2 * count, BLK, HD)
        for b in range(count):
            span = pl.ds(b * BLK, BLK)
            tspan = pl.ds(b * tokens, tokens)
            kb = kh[h, span, :].astype(BF16)
            rs_row = to_row(rsf[h, span, :], eye)
            at = 2 * b * BLK
            ds, ss = split(sd[at + BLK : at + 2 * BLK]), split(sd[at : at + BLK])
            gs = (gsp[h, 0, tspan, :], gsp[h, 1, tspan, :])
            dsc = jnp.where(seen, dot3t(gs, ds), 0.0)
            qg_ref[pl.ds(b * tokens * heads + h, tokens, stride=heads), :] = scale * (
                dot3t(gs, ss) + dot2l(split(dsc * rs_row), kb)
            )
            vh[h, span, :] = dot2l(split(dsc.T * scale), qh[h, tspan, :])
        return carry

    early = (back == 1) & (line <= 1)

    @pl.when(early)
    def first_early():
        lax.fori_loop(0, heads, first_part, 0)

    @pl.when(rank != 0)
    def await_chain():
        chain(1, 0).wait_recv()

    @pl.when(rank == 1)
    def pass_on():
        chain_out[...] = dot3(split(total[:, :HD]), split(entry_in[...])) + total[:, HD:]
        chain(3, 1).start()
        chain(2, 0).start()

    @pl.when(rank == 3)
    def skip_one():
        chain_map().wait_recv()
        entry_in[...] = (
            dot3(split(ahead_map[:, :HD]), split(entry_in[...])) + ahead_map[:, HD:]
        )

    states = split(entry_in[...])
    both[back, home] = dot3(split(pref[home, :, :HD]), states) + pref[home, :, HD:]
    relay(0)

    def finish(step, carry):
        x = lax.rem(home + step, heads)
        entries[x] = dot3(split(pref[x, :, :HD]), states) + pref[x, :, HD:]
        give(x).start()
        return carry

    lax.fori_loop(1, heads, finish, 0)

    @pl.when(jnp.logical_not(early))
    def first_late():
        lax.fori_loop(0, heads, first_part, 0)

    def second_part(turn, carry):
        h = visit(turn)

        @pl.when((back == 1) & (turn + 1 < heads))
        def look_ahead():
            relay(turn + 1)

        @pl.when(back == 0)
        def listen():
            told(h)

        final = split(both[1, h])
        lf = dot3(split(ba[h].reshape(deep, HD)), final) + bb[h].reshape(deep, HD)
        acc = jnp.zeros((8, rows), F32)
        for b in range(count):
            span = pl.ds(b * BLK, BLK)
            kf = kh[h, span, :]
            kt = ktr[h, b]
            rs = rsf[h, span, :]
            beta = btf[h, span, :]
            rs_row = to_row(rs, eye)
            at = 2 * b * BLK
            s0, delta = fb[h, 2 * b], fb[h, 2 * b + 1]
            lam, f = lf[at : at + BLK], lf[at + BLK : at + 2 * BLK]
            e = beta * f
            dlog = jnp.sum(f * delta, axis=1, keepdims=True) * (1.0 - 0.5 * beta)
            dlog = jnp.where(col == row // refl + b * tokens, dlog, 0.0)
            for i in range(BLK // 8):
                acc = acc + dlog[8 * i : 8 * (i + 1), :]
            wide[pl.ds(b * BLK, BLK), :] = e
            ds, es, ss, ls = split(delta), split(e), split(s0), split(lam)
            m = jnp.where(col < row, dot3t(es, ds), 0.0)
            ms = split((m + m.T) * rs_row)
            dk = dg(
                jnp.concatenate([ds[0], ds[1], ds[0]], 1),
                jnp.concatenate([ls[0], ls[0], ls[1]], 1),
                NT,
            ) - dg(
                jnp.concatenate([es[0], es[1], es[0], ms[0], ms[1]], 1),
                jnp.concatenate([ss[0], ss[0], ss[1], kt, kt], 1),
                NT,
            )
            dk = dk + vh[h, span, :]
            ku = kf * rs
            along = jnp.sum(ku * dk, axis=1, keepdims=True)
            wide[pl.ds((count + b) * BLK, BLK), :] = rs * (dk - ku * along)
        for r in range(refl):
            lane = pl.ds(h * refl + r, rows, stride=per_token)
            vg_ref[lane, :] = wide[pl.ds(r, rows, stride=refl), :]
            kg_ref[lane, :] = wide[pl.ds(steps + r, rows, stride=refl), :]
        out = acc[:refl]
        for i in range(1, 8 // refl):
            out = out + acc[i * refl : (i + 1) * refl]
        lgg_ref[h] = out
        return carry

    lax.fori_loop(0, heads, second_part, 0)

    for copy in cot_copies:
        copy.wait_send()
    hand_right.wait_send()
    hand_left.wait_send()
    for h in range(heads):
        hand_over(0, h).wait_send()
        tell(h).wait_send()

    def drain(step, carry):
        x = lax.rem(home + step, heads)
        post(x).wait_send()
        give(x).wait_send()
        return carry

    lax.fori_loop(1, heads, drain, 0)

    @pl.when(rank <= 1)
    def sent_on():
        chain(1, 0).wait_send()

    @pl.when(rank == 1)
    def sent_both():
        chain(3, 1).wait_send()

    @pl.when(rank == 2)
    def sent_map():
        chain_map().wait_send()


def layer(q, k, v, lg, cot, w):
    heads, refl, rows = lg.shape
    steps = rows * refl
    count = steps // BLK
    zsize = lax.axis_size("head")
    dma = pltpu.SemaphoreType.DMA
    vm = pl.BlockSpec(memory_space=pltpu.VMEM)
    saved = pltpu.VMEM((heads, 2 * count, BLK, HD), F32)
    many = pltpu.VMEM((heads, steps, HD), F32)
    aug = pltpu.VMEM((heads, HD, 2 * HD), F32)
    return pl.pallas_call(
        layer_kernel,
        out_shape=(
            jax.ShapeDtypeStruct(q.shape, F32),
            jax.ShapeDtypeStruct(k.shape, F32),
            jax.ShapeDtypeStruct(v.shape, F32),
            jax.ShapeDtypeStruct(lg.shape, F32),
        ),
        in_specs=[vm] * 5 + [pl.BlockSpec(memory_space=pl.ANY)],
        out_specs=(vm,) * 4,
        scratch_shapes=[
            pltpu.VMEM(k.shape, F32),
            many,
            pltpu.VMEM((heads, count, HD, BLK), BF16),
            many,
            pltpu.VMEM((heads, rows, HD), BF16),
            many,
            many,
            pltpu.VMEM((heads, count, 2, BLK, BLK), BF16),
            pltpu.VMEM((heads, count, 2, BLK, BLK), BF16),
            pltpu.VMEM((heads, 2, rows, HD), BF16),
            saved, saved, saved, saved,
            pltpu.VMEM((zsize,) + cot.shape, BF16),
            pltpu.VMEM(w.shape, BF16),
            pltpu.VMEM((2, heads, HD, 2 * HD), F32),
            aug, aug, aug, aug,
            pltpu.VMEM((HD, 2 * HD), F32),
            pltpu.VMEM((HD, HD), F32),
            pltpu.VMEM((HD, 2 * HD), F32),
            pltpu.VMEM((HD, HD), F32),
            pltpu.VMEM((2 * heads, HD, HD), F32),
            pltpu.VMEM((2, heads, HD, HD), F32),
            dma, dma, dma((6,)), dma((6,)),
            dma((heads,)), dma((heads,)), dma((heads,)), dma((heads,)),
            dma((2,)), dma, dma,
            dma((heads,)), dma((heads,)), dma((heads,)), dma((heads,)),
        ],
        compiler_params=pltpu.CompilerParams(collective_id=0, has_side_effects=True),
        name="layer",
    )(q, k, v, lg, cot, w)


def emit_kernel(*refs):
    half = len(refs) // 2
    for source, target in zip(refs[:half], refs[half:]):
        target[...] = source[...]


def emit(q, k, v, lg):
    parts = 4
    specs = [pl.BlockSpec((x.shape[0] // parts,) + x.shape[1:], lambda i: (i, 0)) for x in (q, k, v)]
    specs.append(pl.BlockSpec((lg.shape[0] // parts,) + lg.shape[1:], lambda i: (i, 0, 0)))
    return pl.pallas_call(
        emit_kernel,
        grid=(parts,),
        out_shape=[jax.ShapeDtypeStruct(x.shape, x.dtype) for x in (q, k, v, lg)],
        in_specs=specs,
        out_specs=specs,
        name="emit",
    )(q, k, v, lg)


def local(queries, keys, values, beta_logits, out_cot, out_weight):
    rows, heads, width = queries.shape
    refl = keys.shape[2]
    results = layer(
        queries.reshape(rows * heads, width),
        keys.reshape(rows * heads * refl, width),
        values.reshape(rows * heads * refl, width),
        beta_logits,
        out_cot,
        out_weight,
    )
    query_grad, key_grad, value_grad, beta_grad = emit(*results)
    return (
        query_grad.reshape(queries.shape),
        key_grad.reshape(keys.shape),
        value_grad.reshape(values.shape),
        beta_grad,
    )


def solution(mesh):
    return jax.shard_map(
        local,
        mesh=mesh,
        in_specs=(
            P("seq", "head", None),
            P("seq", "head", None, None),
            P("seq", "head", None, None),
            P("head", None, "seq"),
            P("seq", "head"),
            P("head", None),
        ),
        out_specs=(
            P("seq", "head", None),
            P("seq", "head", None, None),
            P("seq", "head", None, None),
            P("head", None, "seq"),
        ),
        check_vma=False,
    )
```

time: 76.1 us -> 65.1 us (0.86); the launches traced: 75.9 us -> 64 us
  Pallas kernels: 69.6 us -> 63.3 us
  local copies, waits for them, and re-layouts: 5.65 us -> 0 us
    pallas_call x1 -> x2, Pallas kernels: 69.6 us -> 63.3 us  [the longest x1 59.4 us: layer(): pl.pallas_call(layer_kernel, out_shape=(jax.ShapeDtypeStruct(q.shape, F32...]
    transpose x1 -> x0, local copies, waits for them, and re-layouts: 3.22 us -> none  [local(): value_grad = vg.reshape(heads, rows, refl, width).transpose(1, 0, 2, 3)]
    unnamed x4 -> x0, local copies, waits for them, and re-layouts: 2.43 us -> none
where the time goes in v3:
time: 65.1 us; the launch traced here: 64 us
  Pallas kernels  63.3 us (97%)
  between operations  0.72 us (1%)
    pallas_call x1, Pallas kernels, layer(): pl.pallas_call(layer_kernel, out_shape=(jax.ShapeDtypeStruct(q.shape, F32...  59.4 us
    pallas_call x1, Pallas kernels, emit(): pl.pallas_call(emit_kernel, grid=(parts,), out_shape=[jax.ShapeDtypeStruc...  3.88 us

profile of v3, /device:TPU:1, one launch (start us, length us, event | category | flops | bytes accessed | tf_op | source)
XLA Modules:
  0.0 64.0 jit_solution(9944727225143216744)
XLA Ops:
  0.6 59.4 %layer.1 = (f32[512,128]{1,0:T(8,128)}, f32[2048,128]{1,0:T(8,128)}, f32[2048,128]{1,0:T(8,128)}, f32[4,4,128]{2,1,0:T(4,128)}) custom-call(bf16[512,128]{1,0:T(8,128)(2,1)} %bitcast.8, bf16[2048,128]{1,0:T(8,128)(2,1)} %bitcast.6, bf16[2048,128]{1,0:T(8,128)(2,1)} %bitcast.7, f32[4,4,128]{2,1,0:T(4,128)} %lg_ref.1, bf16[128,1024]{1,0:T(8,128)(2,1)} %cot_ref.1, ...), custom_call_target="tpu_custom_call" | custom-call | tf_op jit(solution)/shard_map/layer/pallas_call | solution.py:617
  60.0 3.9 %emit.1 = (f32[512,128]{1,0:T(8,128)}, f32[2048,128]{1,0:T(8,128)}, f32[2048,128]{1,0:T(8,128)}, f32[4,4,128]{2,1,0:T(4,128)}) custom-call(f32[512,128]{1,0:T(8,128)} %get-tuple-element.12.refs_0_, f32[2048,128]{1,0:T(8,128)} %get-tuple-element.13.refs_1_, f32[2048,128]{1,0:T(8,128)} %get-tuple-element.14.refs_2_, f32[4,4,128]{2,1,0:T(4,128)} %get-tuple-element.15.refs_3_), custom_call_target="tpu_custom_call" | custom-call | tf_op jit(solution)/shard_map/emit/pallas_call | solution.py:669

commit v4 on v3

--- a/solution.py
+++ b/solution.py
@@ -109,7 +109,7 @@
 
 def layer_kernel(q_ref, k_ref, v_ref, lg_ref, cot_ref, w_ref,
                  qg_ref, kg_ref, vg_ref, lgg_ref,
-                 wide, kh, ktr, vh, qh, rsf, btf, invn, invt, gsp, fa, fb, ba, bb,
+                 wide, kh, khb, kns, knt, vh, qh, rsf, btf, invn, invt, gsp, fa, fb, ba, bb,
                  full, wbuf, mine, pm, comp, rbuf, pref, total, entry_in, ahead_map, chain_out,
                  entries, both,
                  w_sem, cot_own, cot_send, cot_recv, pm_send, pm_recv, comp_send, comp_recv,
@@ -200,7 +200,7 @@
                 copy.start()
 
         units = [(2 * turn + i, b) for b in range(count) for i in range(2)]
-        lower = []
+        lower, strengths = [], []
         for h, b in units:
             span = pl.ds(b * BLK, BLK)
             kf = kh[h, span, :]
@@ -214,8 +214,14 @@
             rs = jnp.broadcast_to(rs, (BLK, HD))
             beta = jnp.broadcast_to(beta, (BLK, HD))
             rsf[h, span, :] = rs
-            btf[h, span, :] = beta
-            ktr[h, b] = kb.T
+            btf[h, span, :] = 1.0 / beta - 0.5
+            strengths.append(to_row(beta, eye))
+            kn = kf * rs
+            kh[h, span, :] = kn
+            khb[h, span, :] = kb
+            for part, x in enumerate(split(kn)):
+                kns[h, b, part] = x
+                knt[h, b, part] = x.T
             n = jnp.where(col < row, dg(kb, kb, NT) * (rs * beta) * to_row(rs, eye), 0.0)
             lower.append(n)
         spread = []
@@ -227,8 +233,8 @@
         while s < BLK:
             inv = grow_inverse(inv, lower, s, row, col)
             s *= 2
-        for (h, b), x in zip(units, inv):
-            hi, lo = split(x)
+        for (h, b), x, strength in zip(units, inv, strengths):
+            hi, lo = split(x * strength)
             invn[h, b, 0] = hi
             invn[h, b, 1] = lo
             invt[h, b, 0] = hi.T
@@ -268,21 +274,18 @@
         span = pl.ds(b * BLK, BLK)
         for h in range(heads):
             now = state[h]
-            kb = kh[h, span, :].astype(BF16)
-            rs = rsf[h, span, :]
-            beta = btf[h, span, :]
-            moved = dot2(kb, split(now))
-            y = jnp.concatenate(
-                [(-rs * beta) * moved[:, :HD], beta * (vh[h, span, :] - rs * moved[:, HD:])],
-                axis=1,
-            )
+            vb = vh[h, span, :]
+            if b == 0:
+                y = jnp.concatenate([-kh[h, span, :], vb], axis=1)
+            else:
+                moved = dot3((kns[h, b, 0], kns[h, b, 1]), split(now))
+                y = jnp.concatenate([-moved[:, :HD], vb - moved[:, HD:]], axis=1)
             d = dot3((invn[h, b, 0], invn[h, b, 1]), split(y))
             fa[h, 2 * b] = now[:, :HD]
             fb[h, 2 * b] = now[:, HD:]
             fa[h, 2 * b + 1] = d[:, :HD]
             fb[h, 2 * b + 1] = d[:, HD:]
-            rs2 = jnp.concatenate([rs, rs], axis=1)
-            state[h] = now + dot2(ktr[h, b], split(rs2 * d))
+            state[h] = now + dot3((knt[h, b, 0], knt[h, b, 1]), split(d))
     for h in range(heads):
         mine[0, h] = state[h]
 
@@ -330,27 +333,27 @@
             tspan = pl.ds(b * tokens, tokens)
             for i, h in enumerate(pair):
                 now = state[i]
-                kb = kh[h, span, :].astype(BF16)
+                kb = khb[h, span, :]
                 rs = rsf[h, span, :]
-                beta = btf[h, span, :]
                 qb = qh[h, tspan, :]
                 gs = (gsp[h, 0, tspan, :], gsp[h, 1, tspan, :])
                 sc_t = jnp.where(seen_t, dg(kb, qb, NT) * (rs[:, :tokens] * scale), 0.0)
                 direct = dot3(split(sc_t), gs)
-                moved = dot2(kb, split(now))
-                dd = jnp.concatenate([rs * moved[:, :HD], rs * moved[:, HD:] + direct], axis=1)
+                if b == count - 1:
+                    dd = jnp.concatenate([kh[h, span, :], direct], axis=1)
+                else:
+                    moved = dot3((kns[h, b, 0], kns[h, b, 1]), split(now))
+                    dd = jnp.concatenate([moved[:, :HD], moved[:, HD:] + direct], axis=1)
                 f = dot3((invt[h, b, 0], invt[h, b, 1]), split(dd))
                 ba[h, 2 * b] = now[:, :HD]
                 bb[h, 2 * b] = now[:, HD:]
                 ba[h, 2 * b + 1] = f[:, :HD]
                 bb[h, 2 * b + 1] = f[:, HD:]
                 source = dot2(qb.T, gs) * scale
-                rb = rs * beta
-                rb2 = jnp.concatenate([rb, rb], axis=1)
                 state[i] = (
                     now
                     + jnp.concatenate([zero, source], axis=1)
-                    - dot2(ktr[h, b], split(rb2 * f))
+                    - dot3((knt[h, b, 0], knt[h, b, 1]), split(f))
                 )
         for i, h in enumerate(pair):
             mine[1, h] = state[i]
@@ -466,14 +469,12 @@
         for b in range(count):
             span = pl.ds(b * BLK, BLK)
             tspan = pl.ds(b * tokens, tokens)
-            kb = kh[h, span, :].astype(BF16)
-            rs_row = to_row(rsf[h, span, :], eye)
             at = 2 * b * BLK
             ds, ss = split(sd[at + BLK : at + 2 * BLK]), split(sd[at : at + BLK])
             gs = (gsp[h, 0, tspan, :], gsp[h, 1, tspan, :])
             dsc = jnp.where(seen, dot3t(gs, ds), 0.0)
             qg_ref[pl.ds(b * tokens * heads + h, tokens, stride=heads), :] = scale * (
-                dot3t(gs, ss) + dot2l(split(dsc * rs_row), kb)
+                dot3t(gs, ss) + dot3(split(dsc), (kns[h, b, 0], kns[h, b, 1]))
             )
             vh[h, span, :] = dot2l(split(dsc.T * scale), qh[h, tspan, :])
         return carry
@@ -533,34 +534,30 @@
         acc = jnp.zeros((8, rows), F32)
         for b in range(count):
             span = pl.ds(b * BLK, BLK)
-            kf = kh[h, span, :]
-            kt = ktr[h, b]
+            ku = kh[h, span, :]
+            kt = (knt[h, b, 0], knt[h, b, 1])
             rs = rsf[h, span, :]
-            beta = btf[h, span, :]
-            rs_row = to_row(rs, eye)
             at = 2 * b * BLK
             s0, delta = fb[h, 2 * b], fb[h, 2 * b + 1]
-            lam, f = lf[at : at + BLK], lf[at + BLK : at + 2 * BLK]
-            e = beta * f
-            dlog = jnp.sum(f * delta, axis=1, keepdims=True) * (1.0 - 0.5 * beta)
+            lam, e = lf[at : at + BLK], lf[at + BLK : at + 2 * BLK]
+            dlog = jnp.sum(e * delta, axis=1, keepdims=True) * btf[h, span, :]
             dlog = jnp.where(col == row // refl + b * tokens, dlog, 0.0)
             for i in range(BLK // 8):
                 acc = acc + dlog[8 * i : 8 * (i + 1), :]
             wide[pl.ds(b * BLK, BLK), :] = e
             ds, es, ss, ls = split(delta), split(e), split(s0), split(lam)
             m = jnp.where(col < row, dot3t(es, ds), 0.0)
-            ms = split((m + m.T) * rs_row)
+            ms = split(m + m.T)
             dk = dg(
                 jnp.concatenate([ds[0], ds[1], ds[0]], 1),
                 jnp.concatenate([ls[0], ls[0], ls[1]], 1),
                 NT,
             ) - dg(
-                jnp.concatenate([es[0], es[1], es[0], ms[0], ms[1]], 1),
-                jnp.concatenate([ss[0], ss[0], ss[1], kt, kt], 1),
+                jnp.concatenate([es[0], es[1], es[0], ms[0], ms[1], ms[0]], 1),
+                jnp.concatenate([ss[0], ss[0], ss[1], kt[0], kt[0], kt[1]], 1),
                 NT,
             )
             dk = dk + vh[h, span, :]
-            ku = kf * rs
             along = jnp.sum(ku * dk, axis=1, keepdims=True)
             wide[pl.ds((count + b) * BLK, BLK), :] = rs * (dk - ku * along)
         for r in range(refl):
@@ -627,7 +624,9 @@
         scratch_shapes=[
             pltpu.VMEM(k.shape, F32),
             many,
-            pltpu.VMEM((heads, count, HD, BLK), BF16),
+            pltpu.VMEM((heads, steps, HD), BF16),
+            pltpu.VMEM((heads, count, 2, BLK, HD), BF16),
+            pltpu.VMEM((heads, count, 2, HD, BLK), BF16),
             many,
             pltpu.VMEM((heads, rows, HD), BF16),
             many,
@@ -657,23 +656,42 @@
 
 
 def emit_kernel(*refs):
-    half = len(refs) // 2
-    for source, target in zip(refs[:half], refs[half:]):
-        target[...] = source[...]
-
-
-def emit(q, k, v, lg):
+    count = (len(refs) - 2) // 3
+    sources, targets, holds = refs[:count], refs[count : 2 * count], refs[2 * count : 3 * count]
+    in_sem, out_sem = refs[3 * count :]
+    parts = in_sem.shape[1]
+    loads, stores = [], []
+    for p in range(parts):
+        for n in range(count):
+            size = holds[n].shape[0] // parts
+            span = pl.ds(p * size, size)
+            loads.append(
+                pltpu.make_async_copy(sources[n].at[span], holds[n].at[span], in_sem.at[n, p])
+            )
+            stores.append(
+                pltpu.make_async_copy(holds[n].at[span], targets[n].at[span], out_sem.at[n, p])
+            )
+    for load in loads:
+        load.start()
+    for load, store in zip(loads, stores):
+        load.wait()
+        store.start()
+    for store in stores:
+        store.wait()
+
+
+def emit(*arrays):
     parts = 4
-    specs = [pl.BlockSpec((x.shape[0] // parts,) + x.shape[1:], lambda i: (i, 0)) for x in (q, k, v)]
-    specs.append(pl.BlockSpec((lg.shape[0] // parts,) + lg.shape[1:], lambda i: (i, 0, 0)))
+    anywhere = pl.BlockSpec(memory_space=pl.ANY)
     return pl.pallas_call(
         emit_kernel,
-        grid=(parts,),
-        out_shape=[jax.ShapeDtypeStruct(x.shape, x.dtype) for x in (q, k, v, lg)],
-        in_specs=specs,
-        out_specs=specs,
+        out_shape=[jax.ShapeDtypeStruct(x.shape, x.dtype) for x in arrays],
+        in_specs=[anywhere] * len(arrays),
+        out_specs=[anywhere] * len(arrays),
+        scratch_shapes=[pltpu.VMEM(x.shape, x.dtype) for x in arrays]
+        + [pltpu.SemaphoreType.DMA((len(arrays), parts))] * 2,
         name="emit",
-    )(q, k, v, lg)
+    )(*arrays)
 
 
 def local(queries, keys, values, beta_logits, out_cot, out_weight):

time: 65.1 us -> 60 us (0.922)
  Pallas kernels: 63.3 us -> 58.2 us
    pallas_call x1, Pallas kernels: 59.4 us -> 55.6 us  [layer(): pl.pallas_call(layer_kernel, out_shape=(jax.ShapeDtypeStruct(q.shape, F32...]
    pallas_call x1, Pallas kernels: 3.88 us -> 2.65 us  [emit(): pl.pallas_call(emit_kernel, out_shape=[jax.ShapeDtypeStruct(x.shape, x.dt...]
where the time goes in v4:
time: 60 us; the launch traced here: 58.9 us
  Pallas kernels  58.2 us (97%)
  between operations  0.64 us (1%)
    pallas_call x1, Pallas kernels, layer(): pl.pallas_call(layer_kernel, out_shape=(jax.ShapeDtypeStruct(q.shape, F32...  55.6 us
    pallas_call x1, Pallas kernels, emit(): pl.pallas_call(emit_kernel, out_shape=[jax.ShapeDtypeStruct(x.shape, x.dt...  2.65 us

profile of v4, /device:TPU:1, one launch (start us, length us, event | category | flops | bytes accessed | tf_op | source)
XLA Modules:
  0.0 58.9 jit_solution(1466899741254025290)
XLA Ops:
  0.6 55.6 %layer.1 = (f32[512,128]{1,0:T(8,128)}, f32[2048,128]{1,0:T(8,128)}, f32[2048,128]{1,0:T(8,128)}, f32[4,4,128]{2,1,0:T(4,128)}) custom-call(bf16[512,128]{1,0:T(8,128)(2,1)} %bitcast.8, bf16[2048,128]{1,0:T(8,128)(2,1)} %bitcast.6, bf16[2048,128]{1,0:T(8,128)(2,1)} %bitcast.7, f32[4,4,128]{2,1,0:T(4,128)} %lg_ref.1, bf16[128,1024]{1,0:T(8,128)(2,1)} %cot_ref.1, ...), custom_call_target="tpu_custom_call" | custom-call | tf_op jit(solution)/shard_map/layer/pallas_call | solution.py:614
  56.2 2.7 %emit.1 = (f32[512,128]{1,0:T(8,128)}, f32[2048,128]{1,0:T(8,128)}, f32[2048,128]{1,0:T(8,128)}, f32[4,4,128]{2,1,0:T(4,128)}) custom-call(f32[512,128]{1,0:T(8,128)} %get-tuple-element.12.refs_0_, f32[2048,128]{1,0:T(8,128)} %get-tuple-element.13.refs_1_, f32[2048,128]{1,0:T(8,128)} %get-tuple-element.14.refs_2_, f32[4,4,128]{2,1,0:T(4,128)} %get-tuple-element.15.refs_3_), custom_call_target="tpu_custom_call" | custom-call | tf_op jit(solution)/shard_map/emit/pallas_call | solution.py:686
